TPU v7x, 32 devices: a whole 2x2x4 slice. The times are simulated.
32 devices in a mesh: dp: 16 (over z, x, core), tensor: 2 (over y).
Axes of the slice: x: 2, y: 2, z: 4, core: 2. Of those that a mesh axis runs over, the one named last changes fastest.
Arguments:
- inputs: bfloat16 [16384, 768], P(('dp', 'tensor')), may hold values from -6 to 6
- teacher: bfloat16 [16384, 768], P(('dp', 'tensor')), may hold values from -6 to 6
- lengths: int32 [16], P('dp'), may hold values from 256 to 1024
- w_query: bfloat16 [768, 768], P(('tensor', 'dp')), may hold values from -0.3125 to 0.3125
- w_key: bfloat16 [768, 768], P(('tensor', 'dp')), may hold values from -0.3125 to 0.3125
- w_value: bfloat16 [768, 768], P(('tensor', 'dp')), may hold values from -0.21875 to 0.21875
- w_out: bfloat16 [768, 768], P(('tensor', 'dp')), may hold values from -1.25 to 1.25
- w_up: bfloat16 [3072, 768], P(('tensor', 'dp')), may hold values from -0.21875 to 0.21875
- w_down: bfloat16 [3072, 768], P(('tensor', 'dp')), may hold values from -0.21875 to 0.21875
- b_query: float32 [768], replicated, may hold values from -3 to 3
- b_value: float32 [768], replicated, may hold values from -1.25 to 1.25
- b_out: float32 [768], replicated, may hold values from -1.75 to 1.75
- b_up: float32 [3072], replicated, may hold values from -3 to 3
- b_down: float32 [768], replicated, may hold values from -1.75 to 1.75
- gain_one: float32 [768], replicated, may hold values from 0.5 to 1.5
- shift_one: float32 [768], replicated, may hold values from -1.75 to 1.75
- gain_two: float32 [768], replicated, may hold values from 0.5 to 1.5
- shift_two: float32 [768], replicated, may hold values from -1.75 to 1.75
- z_head: float32 [12], replicated, may hold values from 0.4 to 1
- z_mha: float32 [1], replicated, may hold values from 0.4 to 1
- z_hidden: float32 [768], replicated, may hold values from 0.4 to 1
- z_int: float32 [3072], replicated, may hold values from 0.4 to 1
- z_ffn: float32 [1], replicated, may hold values from 0.4 to 1
Outputs:
- layer_out: float32 [16384, 768], P(('dp', 'tensor'))
- loss_value: float32 [1], replicated
- grad_inputs: float32 [16384, 768], P(('dp', 'tensor'))
- grad_w_query: float32 [768, 768], P(('tensor', 'dp'))
- grad_w_key: float32 [768, 768], P(('tensor', 'dp'))
- grad_w_value: float32 [768, 768], P(('tensor', 'dp'))
- grad_w_out: float32 [768, 768], P(('tensor', 'dp'))
- grad_w_up: float32 [3072, 768], P(('tensor', 'dp'))
- grad_w_down: float32 [3072, 768], P(('tensor', 'dp'))
- grad_b_query: float32 [768], replicated
- grad_b_value: float32 [768], replicated
- grad_b_out: float32 [768], replicated
- grad_b_up: float32 [3072], replicated
- grad_b_down: float32 [768], replicated
- grad_gain_one: float32 [768], replicated
- grad_shift_one: float32 [768], replicated
- grad_gain_two: float32 [768], replicated
- grad_shift_two: float32 [768], replicated
- grad_z_head: float32 [12], replicated
- grad_z_mha: float32 [1], replicated
- grad_z_hidden: float32 [768], replicated
- grad_z_int: float32 [3072], replicated
- grad_z_ffn: float32 [1], replicated
All inputs are finite; a program needn't handle non-finite values.
Results may differ from a plain program's by a relative error of at most 0.013.
The roundings to bfloat16 on the way count: a program that leaves them out, or rounds other values in their place, can miss the bound.
Values may be sent and summed in bfloat16 or wider, within the bound.
A program may use at most 192 MiB of HBM per device.

v0:
```python
import math

import jax
import jax.numpy as jnp
from jax import lax
from jax.sharding import PartitionSpec as P

D = 768
HEADS = 12
FF = 3072
SEQ = 1024


epsilon = 1e-12


def norm_rows(summed, gain_vec, shift_vec):
    average = jnp.mean(summed, axis=-1, keepdims=True)
    centered = summed - average
    variance = jnp.mean(centered * centered, axis=-1, keepdims=True)
    return centered * lax.rsqrt(variance + epsilon) * gain_vec + shift_vec


def gelu_exact(values):
    return jax.nn.gelu(values, approximate=False)


def times_plain(left, right):
    return jnp.dot(left, right, preferred_element_type=jnp.float32)


def times_trans(left, right):
    return lax.dot_general(
        left, right, (((1,), (1,)), ((), ())), preferred_element_type=jnp.float32
    )


def trans_times(left, right):
    return lax.dot_general(
        left, right, (((0,), (0,)), ((), ())), preferred_element_type=jnp.float32
    )


def gather_attn(w_query, w_key, w_value, w_out):
    return (
        lax.all_gather(w_query, "dp", axis=0, tiled=True),
        lax.all_gather(w_key, "dp", axis=0, tiled=True),
        lax.all_gather(w_value, "dp", axis=0, tiled=True),
        lax.all_gather(w_out, "dp", axis=0, tiled=True),
    )


def gather_ffn(w_up, w_down):
    return (
        lax.all_gather(w_up, "dp", axis=0, tiled=True),
        lax.all_gather(w_down, "dp", axis=0, tiled=True),
    )


def spread_into(local_vec, full_len, offset):
    return lax.dynamic_update_slice(jnp.zeros((full_len,), jnp.float32), local_vec, (offset,))


def on_device(
    inputs,
    teacher,
    lengths,
    w_query,
    w_key,
    w_value,
    w_out,
    w_up,
    w_down,
    b_query,
    b_value,
    b_out,
    b_up,
    b_down,
    gain_one,
    shift_one,
    gain_two,
    shift_two,
    z_head,
    z_mha,
    z_hidden,
    z_int,
    z_ffn,
):
    rows_own = inputs.shape[0]
    tensor_pos = lax.axis_index("tensor")
    tensor_count = lax.axis_size("tensor")
    group_rows = rows_own * tensor_count
    seq_count = group_rows // SEQ
    head_size = D // HEADS
    local_width = D // tensor_count
    heads_local = local_width // head_size
    units_local = FF // tensor_count
    qblock = min(512, SEQ)
    nblocks = SEQ // qblock
    softmax_scale = 1.0 / math.sqrt(head_size)
    positions = jnp.arange(group_rows, dtype=jnp.int32)
    seq_of_row = positions // SEQ
    picks = seq_of_row[:, None] == jnp.arange(seq_count, dtype=jnp.int32)[None, :]
    row_length = jnp.sum(jnp.where(picks, lengths[None, :], 0), axis=1)
    valid_group = positions % SEQ < row_length
    valid_own = lax.dynamic_slice_in_dim(valid_group, tensor_pos * rows_own, rows_own)
    head_start = tensor_pos * local_width
    unit_start = tensor_pos * units_local
    bias_query = lax.dynamic_slice_in_dim(b_query, head_start, local_width)
    bias_value = lax.dynamic_slice_in_dim(b_value, head_start, local_width)
    gate_heads = lax.dynamic_slice_in_dim(z_head, tensor_pos * heads_local, heads_local)
    bias_up = lax.dynamic_slice_in_dim(b_up, unit_start, units_local)
    gate_units = lax.dynamic_slice_in_dim(z_int, unit_start, units_local)
    wq_full, wk_full, wv_full, wo_full = gather_attn(w_query, w_key, w_value, w_out)
    x_group = lax.all_gather(inputs, "tensor", axis=0, tiled=True)
    query = ((times_trans(x_group, wq_full) + bias_query) * softmax_scale).astype(jnp.bfloat16)
    keys_b = times_trans(x_group, wk_full).astype(jnp.bfloat16)
    values_b = (times_trans(x_group, wv_full) + bias_value).astype(jnp.bfloat16)
    query5 = query.reshape(seq_count, nblocks, qblock, heads_local, head_size)
    keys4 = keys_b.reshape(seq_count, SEQ, heads_local, head_size)
    values4 = values_b.reshape(seq_count, SEQ, heads_local, head_size)
    valid2 = valid_group.reshape(seq_count, SEQ)

    def forward_seq(element):
        query_seq, keys_seq, values_seq, key_valid = element

        def forward_block(query_blk):
            scores = jnp.einsum(
                "qhd,khd->hqk", query_blk, keys_seq, preferred_element_type=jnp.float32
            )
            scores = jnp.where(key_valid[None, None, :], scores, -1e30)
            highest = jnp.max(scores, axis=-1, keepdims=True)
            exponent = jnp.exp(scores - highest)
            denominator = jnp.sum(exponent, axis=-1, keepdims=True)
            attention = (exponent / denominator).astype(jnp.bfloat16)
            context = jnp.einsum(
                "hqk,khd->qhd", attention, values_seq, preferred_element_type=jnp.float32
            )
            return (context, (highest + jnp.log(denominator))[..., 0])

        return lax.map(forward_block, query_seq)

    context_all, logsum_all = lax.map(forward_seq, (query5, keys4, values4, valid2))
    context_f = context_all.reshape(group_rows, heads_local, head_size)
    gated = (
        (context_f * gate_heads[None, :, None])
        .reshape(group_rows, local_width)
        .astype(jnp.bfloat16)
    )
    attn_out = (
        lax.psum_scatter(times_plain(gated, wo_full), "tensor", scatter_dimension=0, tiled=True)
        + b_out
    )
    branch_attn = z_mha * z_hidden
    first_sum = inputs.astype(jnp.float32) + branch_attn * attn_out
    first_norm = norm_rows(first_sum, gain_one, shift_one)
    y_group = lax.all_gather(first_norm.astype(jnp.bfloat16), "tensor", axis=0, tiled=True)
    wu_full, wd_full = gather_ffn(w_up, w_down)
    upper = times_trans(y_group, wu_full) + bias_up
    activated = gelu_exact(upper)
    hidden_b = (activated * gate_units).astype(jnp.bfloat16)
    down = (
        lax.psum_scatter(times_plain(hidden_b, wd_full), "tensor", scatter_dimension=0, tiled=True)
        + b_down
    )
    branch_ffn = z_ffn * z_hidden
    second_sum = first_norm + branch_ffn * down
    output = norm_rows(second_sum, gain_two, shift_two)
    residue = output - teacher.astype(jnp.float32)
    masked = jnp.where(valid_own[:, None], residue, 0.0)
    valid_count, square_sum = lax.psum(
        (jnp.sum(valid_own.astype(jnp.float32)), jnp.sum(masked * masked)), ("dp", "tensor")
    )
    loss_value = square_sum / (D * valid_count)
    tokens_all = group_rows * lax.axis_size("dp")
    grad_out = masked * (2.0 * tokens_all / valid_count)
    ffn_back = gather_ffn(w_up, w_down)
    attn_back = gather_attn(w_query, w_key, w_value, w_out)
    unused, pull_two = jax.vjp(norm_rows, second_sum, gain_two, shift_two)
    grad_second, grad_gain_two, grad_shift_two = pull_two(grad_out)
    grad_down = (grad_second * branch_ffn).astype(jnp.bfloat16)
    grad_z_ffn = jnp.sum(grad_second * z_hidden * down).reshape(1)
    hidden_part = jnp.sum(grad_second * z_ffn * down, axis=0)
    grad_b_down = jnp.sum(grad_down.astype(jnp.float32), axis=0)
    down_group = lax.all_gather(grad_down, "tensor", axis=0, tiled=True)
    grad_w_down = trans_times(hidden_b, down_group)
    grad_hidden = times_trans(down_group, ffn_back[1])
    grad_z_int_local = jnp.sum(grad_hidden * activated, axis=0)
    unused, gelu_pull = jax.vjp(gelu_exact, upper)
    grad_upper = gelu_pull(grad_hidden * gate_units)[0].astype(jnp.bfloat16)
    grad_b_up_local = jnp.sum(grad_upper.astype(jnp.float32), axis=0)
    grad_w_up = trans_times(grad_upper, y_group)
    grad_first_norm = grad_second + lax.psum_scatter(
        times_plain(grad_upper, ffn_back[0]), "tensor", scatter_dimension=0, tiled=True
    )
    unused, pull_one = jax.vjp(norm_rows, first_sum, gain_one, shift_one)
    grad_first, grad_gain_one, grad_shift_one = pull_one(grad_first_norm)
    grad_attn = (grad_first * branch_attn).astype(jnp.bfloat16)
    grad_z_mha = jnp.sum(grad_first * z_hidden * attn_out).reshape(1)
    hidden_part = hidden_part + jnp.sum(grad_first * z_mha * attn_out, axis=0)
    grad_b_out = jnp.sum(grad_attn.astype(jnp.float32), axis=0)
    attn_group = lax.all_gather(grad_attn, "tensor", axis=0, tiled=True)
    grad_w_out = trans_times(gated, attn_group)
    grad_gated = times_trans(attn_group, attn_back[3]).reshape(group_rows, heads_local, head_size)
    grad_z_head_local = jnp.sum(grad_gated * context_f, axis=(0, 2))
    grad_heads = (grad_gated * gate_heads[None, :, None]).astype(jnp.bfloat16)
    grad_heads5 = grad_heads.reshape(seq_count, nblocks, qblock, heads_local, head_size)

    def backward_seq(element):
        query_seq, keys_seq, values_seq, key_valid, grad_seq, logsum_seq = element
        initial = jnp.zeros((SEQ, heads_local, head_size), jnp.float32)

        def backward_block(running, block):
            keys_acc, values_acc = running
            query_blk, grad_blk, logsum_blk = block
            scores = jnp.einsum(
                "qhd,khd->hqk", query_blk, keys_seq, preferred_element_type=jnp.float32
            )
            scores = jnp.where(key_valid[None, None, :], scores, -1e30)
            attention = jnp.exp(scores - logsum_blk[..., None])
            attention_b = attention.astype(jnp.bfloat16)
            grad_attention = jnp.einsum(
                "qhd,khd->hqk", grad_blk, values_seq, preferred_element_type=jnp.float32
            )
            row_dots = jnp.sum(attention * grad_attention, axis=-1, keepdims=True)
            grad_scores = (attention * (grad_attention - row_dots)).astype(jnp.bfloat16)
            grad_query_blk = (
                softmax_scale
                * jnp.einsum(
                    "hqk,khd->qhd", grad_scores, keys_seq, preferred_element_type=jnp.float32
                )
            ).astype(jnp.bfloat16)
            keys_acc = keys_acc + jnp.einsum(
                "hqk,qhd->khd", grad_scores, query_blk, preferred_element_type=jnp.float32
            )
            values_acc = values_acc + jnp.einsum(
                "hqk,qhd->khd", attention_b, grad_blk, preferred_element_type=jnp.float32
            )
            return ((keys_acc, values_acc), grad_query_blk)

        (keys_acc, values_acc), grad_query_seq = lax.scan(
            backward_block, (initial, initial), (query_seq, grad_seq, logsum_seq)
        )
        return (grad_query_seq, keys_acc.astype(jnp.bfloat16), values_acc.astype(jnp.bfloat16))

    grad_query_all, grad_keys_all, grad_values_all = lax.map(
        backward_seq, (query5, keys4, values4, valid2, grad_heads5, logsum_all)
    )
    grad_query = grad_query_all.reshape(group_rows, local_width)
    grad_keys = grad_keys_all.reshape(group_rows, local_width)
    grad_values = grad_values_all.reshape(group_rows, local_width)
    grad_w_query = trans_times(grad_query, x_group)
    grad_w_key = trans_times(grad_keys, x_group)
    grad_w_value = trans_times(grad_values, x_group)
    grad_b_query_local = jnp.sum(grad_query.astype(jnp.float32), axis=0)
    grad_b_value_local = jnp.sum(grad_values.astype(jnp.float32), axis=0)
    part_query = times_plain(grad_query, attn_back[0])
    part_keys = times_plain(grad_keys, attn_back[1])
    part_values = times_plain(grad_values, attn_back[2])
    grad_inputs = grad_first + lax.psum_scatter(
        (part_query + part_keys + part_values).astype(jnp.bfloat16),
        "tensor",
        scatter_dimension=0,
        tiled=True,
    ).astype(jnp.float32)
    shard_wq, shard_wk, shard_wv, shard_wo, shard_wu, shard_wd = (
        lax.psum_scatter(grad_w_query, "dp", scatter_dimension=0, tiled=True),
        lax.psum_scatter(grad_w_key, "dp", scatter_dimension=0, tiled=True),
        lax.psum_scatter(grad_w_value, "dp", scatter_dimension=0, tiled=True),
        lax.psum_scatter(grad_w_out, "dp", scatter_dimension=0, tiled=True),
        lax.psum_scatter(grad_w_up, "dp", scatter_dimension=0, tiled=True),
        lax.psum_scatter(grad_w_down, "dp", scatter_dimension=0, tiled=True),
    )
    small_sums = lax.psum(
        (
            spread_into(grad_b_query_local, D, head_start),
            spread_into(grad_b_value_local, D, head_start),
            grad_b_out,
            spread_into(grad_b_up_local, FF, unit_start),
            grad_b_down,
            grad_gain_one,
            grad_shift_one,
            grad_gain_two,
            grad_shift_two,
            spread_into(grad_z_head_local, HEADS, tensor_pos * heads_local),
            grad_z_mha,
            hidden_part,
            spread_into(grad_z_int_local, FF, unit_start),
            grad_z_ffn,
        ),
        ("dp", "tensor"),
    )
    return (
        output,
        loss_value.reshape(1),
        grad_inputs,
        shard_wq,
        shard_wk,
        shard_wv,
        shard_wo,
        shard_wu,
        shard_wd,
        small_sums[0],
        small_sums[1],
        small_sums[2],
        small_sums[3],
        small_sums[4],
        small_sums[5],
        small_sums[6],
        small_sums[7],
        small_sums[8],
        small_sums[9],
        small_sums[10],
        small_sums[11],
        small_sums[12],
        small_sums[13],
    )


def solution(mesh):
    return jax.shard_map(
        on_device,
        mesh=mesh,
        in_specs=(
            P(("dp", "tensor"), None),
            P(("dp", "tensor"), None),
            P("dp"),
            P(("tensor", "dp"), None),
            P(("tensor", "dp"), None),
            P(("tensor", "dp"), None),
            P(("tensor", "dp"), None),
            P(("tensor", "dp"), None),
            P(("tensor", "dp"), None),
            P(),
            P(),
            P(),
            P(),
            P(),
            P(),
            P(),
            P(),
            P(),
            P(),
            P(),
            P(),
            P(),
            P(),
        ),
        out_specs=(
            P(("dp", "tensor"), None),
            P(),
            P(("dp", "tensor"), None),
            P(("tensor", "dp"), None),
            P(("tensor", "dp"), None),
            P(("tensor", "dp"), None),
            P(("tensor", "dp"), None),
            P(("tensor", "dp"), None),
            P(("tensor", "dp"), None),
            P(),
            P(),
            P(),
            P(),
            P(),
            P(),
            P(),
            P(),
            P(),
            P(),
            P(),
            P(),
            P(),
            P(),
        ),
        check_vma=False,
    )
```

profile of v0, /device:TPU:6, one launch (start us, length us, event | category | flops | bytes accessed | tf_op | source)
XLA Modules:
  0.0 963.0 jit_solution(14815683385056874799)
XLA Ops:
  11.3 19.8 %all_gather.37 = bf16[384,768]{1,0:T(8,128)(2,1)S(1)} all-gather(bf16[24,768]{1,0:T(8,128)(2,1)} %param.30), channel_id=1, replica_groups=mesh['dp'=16,'tensor'=2] {'dp'}, dimensions={0}, use_global_device_ids=true | all-gather | bytes 626688 | tf_op jit(solution)/shard_map/all_gather | solution.py:46
  31.0 23.3 %all_gather.38 = bf16[384,768]{1,0:T(8,128)(2,1)S(1)} all-gather(bf16[24,768]{1,0:T(8,128)(2,1)} %param.31), channel_id=1, replica_groups=mesh['dp'=16,'tensor'=2] {'dp'}, dimensions={0}, use_global_device_ids=true | all-gather | bytes 626688 | tf_op jit(solution)/shard_map/all_gather | solution.py:47
  54.3 19.0 %all_gather.39 = bf16[384,768]{1,0:T(8,128)(2,1)S(1)} all-gather(bf16[24,768]{1,0:T(8,128)(2,1)S(1)} %copy-done.31), channel_id=1, replica_groups=mesh['dp'=16,'tensor'=2] {'dp'}, dimensions={0}, use_global_device_ids=true | all-gather | bytes 626688 | tf_op jit(solution)/shard_map/all_gather | solution.py:48
  73.4 21.9 %all_gather.40 = bf16[384,768]{1,0:T(8,128)(2,1)} all-gather(bf16[24,768]{1,0:T(8,128)(2,1)S(1)} %copy-done.32), channel_id=1, replica_groups=mesh['dp'=16,'tensor'=2] {'dp'}, dimensions={0}, use_global_device_ids=true | all-gather | bytes 626688 | tf_op jit(solution)/shard_map/all_gather | solution.py:49
  101.7 48.4 %while.48 = (s32[]{:T(128)}, f32[2,512,6,64]{1,0,3,2:T(2,128)}, f32[2,6,512]{2,1,0:T(8,128)S(1)}, bf16[2,512,6,64]{1,3,2,0:T(8,128)(2,1)S(1)}, bf16[1024,6,64]{0...) while((s32[]{:T(128)}, f32[2,512,6,64]{1,0,3,2:T(2,128)}, ...), condition=%wide.region_3.4_spmd.clone, body=%wide.region_0.3_spmd.clone.sunk | while | flops 833630208 | bytes 43761780 | solution.py:141
  104.3 2.8 fusion.145
  107.1 3.0 fusion.146
  110.9 15.0 %dynamic_update_slice.55 = f32[2,512,6,64]{1,0,3,2:T(2,128)} dynamic-update-slice(f32[2,512,6,64]{1,0,3,2:T(2,128)} %get-tuple-element.493, f32[1,512,6,64]{1,0,3,2:T(1,128)S(1)} %copy.97, s32[]{:T(128)S(6)} %copy.104, s32[]{:T(128)} %constant.77.clone.1..sunk, s32[]{:T(128)} %constant.77.clone.1..sunk, s32[]{:T(128)} %constant.77.clone.1..sunk) | dynamic-update-slice | bytes 1572868 | tf_op jit(solution)/shard_map/while/body/eval_jaxpr/while/body/jit(dynamic_update_index_in_dim)/dynamic_update_slice | solution.py:141
  128.5 2.8 fusion.145
  131.3 3.0 fusion.146
  135.1 15.0 %dynamic_update_slice.55 = f32[2,512,6,64]{1,0,3,2:T(2,128)} dynamic-update-slice(f32[2,512,6,64]{1,0,3,2:T(2,128)} %get-tuple-element.493, f32[1,512,6,64]{1,0,3,2:T(1,128)S(1)} %copy.97, s32[]{:T(128)S(6)} %copy.104, s32[]{:T(128)} %constant.77.clone.1..sunk, s32[]{:T(128)} %constant.77.clone.1..sunk, s32[]{:T(128)} %constant.77.clone.1..sunk) | dynamic-update-slice | bytes 1572868 | tf_op jit(solution)/shard_map/while/body/eval_jaxpr/while/body/jit(dynamic_update_index_in_dim)/dynamic_update_slice | solution.py:141
  157.9 38.5 %reduce-scatter.11.cloned.1.call-done = f32[512,768]{1,0:T(8,128)} async-done(((f32[1024,768]{1,0:T(8,128)}), f32[512,768]{1,0:T(8,128)}) %reduce-scatter.11.cloned.1.call-update) | async-done | bytes 1572880 | tf_op jit(solution)/shard_map/reduce_scatter | solution.py:151
  201.0 26.3 %all-gather.9.cloned.1.call-done = bf16[1024,768]{1,0:T(8,128)(2,1)} async-done(((bf16[512,768]{1,0:T(8,128)(2,1)}), bf16[1024,768]{1,0:T(8,128)(2,1)}) %all-gather.9.cloned.1.call-update) | async-done | bytes 1572880 | tf_op jit(solution)/shard_map/all_gather | solution.py:157
  227.4 20.1 %multiply_convert_fusion.1 = (bf16[1024,1536]{1,0:T(8,128)(2,1)}, f32[1024,1536]{1,0:T(8,128)}, f32[1024,1536]{1,0:T(8,128)}) fusion(f32[1536]{0:T(1024)S(1)} %dynamic_slice.60, f32[1536]{0:T(1024)S(1)} %dynamic_slice.59, bf16[1024,768]{1,0:T(8,128)(2,1)} %all-gather.9.cloned.1.call-done, bf16[1536,768]{1,0:T(8,128)(2,1)} %all-gather.11.cloned.1.call-done), kind=kOutput, calls=%fused_computation.73 | convolution fusion | flops 2521300992 | bytes 19673088 | tf_op jit(solution)/shard_map/dot_general | solution.py:33
  247.5 25.1 %all-gather.13.cloned.1.call-done = bf16[1536,768]{1,0:T(8,128)(2,1)} async-done(((bf16[96,768]{1,0:T(8,128)(2,1)}), bf16[1536,768]{1,0:T(8,128)(2,1)}) %all-gather.13.cloned.1.call-update) | async-done | bytes 2359312 | tf_op jit(solution)/shard_map/all_gather | solution.py:56
  272.5 6.9 fusion.75
  280.8 40.7 %psum.113 = f32[]{:T(128)} all-reduce(f32[]{:T(128)} %get-tuple-element.352), channel_id=1, replica_groups=mesh['dp'=16,'tensor'=2] {'dp','tensor'}, use_global_device_ids=true, to_apply=%region_13.14 | all-reduce | flops 1 | bytes 8 | tf_op jit(solution)/shard_map/psum | solution.py:171
  325.7 2.8 multiply_reduce_fusion.7
  332.0 27.2 %all-gather.15.cloned.1.call-done = bf16[1024,768]{1,0:T(8,128)(2,1)} async-done(((bf16[512,768]{1,0:T(8,128)(2,1)}), bf16[1024,768]{1,0:T(8,128)(2,1)}) %all-gather.15.cloned.1.call-update) | async-done | bytes 1572880 | tf_op jit(solution)/shard_map/all_gather | solution.py:185
  359.2 10.6 %convert_reduce_fusion = (f32[1536]{0:T(1024)}, bf16[1024,1536]{1,0:T(8,128)(2,1)S(1)}, f32[1536]{0:T(1024)}) fusion(f32[1024,1536]{1,0:T(8,128)} %get-tuple-element.357, f32[1536]{0:T(1024)S(1)} %dynamic_slice.60, f32[1024,1536]{1,0:T(8,128)} %get-tuple-element.368, f32[1536]{0:T(1024)S(1)} %dynamic_slice.59, ...), kind=kOutput, calls=%fused_computation.71 | convolution fusion | flops 2448946176 | bytes 19685376 | tf_op jit(solution)/shard_map/dot_general | solution.py:33
  371.4 4.2 fusion.76
  375.7 43.3 %reduce-scatter.15.cloned.1.call-done = f32[512,768]{1,0:T(8,128)} async-done(((f32[1024,768]{1,0:T(8,128)}), f32[512,768]{1,0:T(8,128)}) %reduce-scatter.15.cloned.1.call-update) | async-done | bytes 1572880 | tf_op jit(solution)/shard_map/reduce_scatter | solution.py:193
  419.1 3.3 multiply_reduce_fusion.8
  427.9 25.4 %all-gather.17.cloned.1.call-done = bf16[1024,768]{1,0:T(8,128)(2,1)} async-done(((bf16[512,768]{1,0:T(8,128)(2,1)}), bf16[1024,768]{1,0:T(8,128)(2,1)}) %all-gather.17.cloned.1.call-update) | async-done | bytes 1572880 | tf_op jit(solution)/shard_map/all_gather | solution.py:202
  453.3 4.8 multiply_reduce_fusion.6
  464.7 48.7 %while.49 = (s32[]{:T(128)}, f32[1024,6,64]{0,2,1:T(8,128)S(1)}, f32[1024,6,64]{0,2,1:T(8,128)}, bf16[2,512,6,64]{1,3,2,0:T(8,128)(2,1)}, bf16[2,512,6,64]{1,3,2...) while((s32[]{:T(128)}, f32[1024,6,64]{0,2,1:T(8,128)S(1)}, ...), condition=%wide.region_21.22_spmd.clone, body=%wide.region_19.21_spmd.clone.sunk | while | flops 2052993024 | bytes 142831920 | solution.py:241
  465.4 2.8 fusion.156
  468.3 3.5 bitcast_add_fusion.5
  471.8 4.6 multiply_reduce_fusion.16
  476.4 4.6 multiply_convert_fusion.12
  481.0 5.9 fusion.158
  489.1 2.8 fusion.156
  491.9 4.6 bitcast_add_fusion.5
  496.6 4.6 multiply_reduce_fusion.16
  501.2 4.6 multiply_convert_fusion.12
  505.8 5.9 fusion.158
  523.7 6.7 fusion.83
  531.8 6.7 fusion.82
  542.4 3.6 fusion.81
  548.3 3.3 fusion.79
  555.6 5.1 multiply_reduce_fusion.3
  560.7 43.9 %all-reduce = (f32[]{:T(128)}, f32[768]{0:T(1024)}, f32[768]{0:T(1024)}, f32[768]{0:T(1024)}, f32[3072]{0:T(1024)}, /*index=5*/f32[768]{0:T(1024)}, f32[768]{0:T...) all-reduce(f32[]{:T(128)} %get-tuple-element.284, ...), channel_id=1, replica_groups=mesh['dp'=16,'tensor'=2] {'dp','tensor'}, use_global_device_ids=true, to_apply=%region_11.12 | all-reduce | flops 13071 | bytes 104568 | tf_op jit(solution)/shard_map/psum | solution.py:171
  605.3 23.6 %reduce-scatter.29.cloned.1.call-done = f32[96,768]{1,0:T(8,128)} async-done(((f32[1536,768]{1,0:T(8,128)}), f32[96,768]{1,0:T(8,128)}) %reduce-scatter.29.cloned.1.call-update) | async-done | bytes 294928 | tf_op jit(solution)/shard_map/reduce_scatter | solution.py:272
  628.9 79.6 %reduce-scatter.27.cloned.1.call-done = f32[96,768]{1,0:T(8,128)} async-done(((f32[1536,768]{1,0:T(8,128)}), f32[96,768]{1,0:T(8,128)}) %reduce-scatter.27.cloned.1.call-update) | async-done | bytes 294928 | tf_op jit(solution)/shard_map/reduce_scatter | solution.py:271
  708.5 61.9 %reduce-scatter.25.cloned.1.call-done = f32[24,768]{1,0:T(8,128)} async-done(((f32[384,768]{1,0:T(8,128)}), f32[24,768]{1,0:T(8,128)}) %reduce-scatter.25.cloned.1.call-update) | async-done | bytes 73744 | tf_op jit(solution)/shard_map/reduce_scatter | solution.py:270
  770.4 61.3 %reduce-scatter.23.cloned.1.call-done = f32[24,768]{1,0:T(8,128)} async-done(((f32[384,768]{1,0:T(8,128)}), f32[24,768]{1,0:T(8,128)}) %reduce-scatter.23.cloned.1.call-update) | async-done | bytes 73744 | tf_op jit(solution)/shard_map/reduce_scatter | solution.py:269
  831.7 61.1 %reduce-scatter.21.cloned.1.call-done = f32[24,768]{1,0:T(8,128)} async-done(((f32[384,768]{1,0:T(8,128)}), f32[24,768]{1,0:T(8,128)}) %reduce-scatter.21.cloned.1.call-update) | async-done | bytes 73744 | tf_op jit(solution)/shard_map/reduce_scatter | solution.py:268
  892.8 61.3 %reduce-scatter.19.cloned.1.call-done = f32[24,768]{1,0:T(8,128)} async-done(((f32[384,768]{1,0:T(8,128)}), f32[24,768]{1,0:T(8,128)}) %reduce-scatter.19.cloned.1.call-update) | async-done | bytes 73744 | tf_op jit(solution)/shard_map/reduce_scatter | solution.py:267
  (264 shorter events, 73.6 us)
Async XLA Ops:
  8.0 46.3 %copy-start.31 = (bf16[24,768]{1,0:T(8,128)(2,1)S(1)}, bf16[24,768]{1,0:T(8,128)(2,1)}, u32[]{:S(2)}) copy-start(bf16[24,768]{1,0:T(8,128)(2,1)} %param.32) | copy-start | bytes 110596
  8.0 65.3 %copy-start.32 = (bf16[24,768]{1,0:T(8,128)(2,1)S(1)}, bf16[24,768]{1,0:T(8,128)(2,1)}, u32[]{:S(2)}) copy-start(bf16[24,768]{1,0:T(8,128)(2,1)} %param.33) | copy-start | bytes 110596
  8.0 87.3 %all-gather.7.cloned.1.call-start = ((), (), s32[]{:S(2)}) async-start(), calls=%async_computation.10 | async-start | bytes 2359296 | tf_op jit(solution)/shard_map/all_gather | solution.py:115
  8.8 187.6 %reduce-scatter.11.cloned.1.call-start = ((), (), s32[]{:S(2)}) async-start(), calls=%async_computation.11 | async-start | bytes 4718592 | tf_op jit(solution)/shard_map/reduce_scatter | solution.py:151
  11.1 86.6 %copy-start.59 = (f32[6]{0:T(128)}, f32[6]{0:T(128)S(1)}, u32[]{:S(2)}) copy-start(f32[6]{0:T(128)S(1)} %dynamic_slice.58) | copy-start | bytes 76
  11.3 141.5 %copy-start.35 = (f32[384]{0:T(512)}, f32[384]{0:T(512)S(1)}, u32[]{:S(2)}) copy-start(f32[384]{0:T(512)S(1)} %mul.331) | copy-start | bytes 4612
  31.0 64.3 %copy-start.23 = (bf16[384,768]{1,0:T(8,128)(2,1)}, bf16[384,768]{1,0:T(8,128)(2,1)S(1)}, u32[]{:S(2)}) copy-start(bf16[384,768]{1,0:T(8,128)(2,1)S(1)} %all_gather.37) | copy-start | bytes 1769476
  54.3 44.4 %copy-start.27 = (bf16[384,768]{1,0:T(8,128)(2,1)}, bf16[384,768]{1,0:T(8,128)(2,1)S(1)}, u32[]{:S(2)}) copy-start(bf16[384,768]{1,0:T(8,128)(2,1)S(1)} %all_gather.38) | copy-start | bytes 1769476
  73.4 27.5 %copy-start.25 = (bf16[384,768]{1,0:T(8,128)(2,1)}, bf16[384,768]{1,0:T(8,128)(2,1)S(1)}, u32[]{:S(2)}) copy-start(bf16[384,768]{1,0:T(8,128)(2,1)S(1)} %all_gather.39) | copy-start | bytes 1769476
  150.1 5.5 copy-start.1
  150.1 5.5 copy-start.4
  152.8 273.4 %copy-start.8 = (f32[48,8,2,512]{3,1,2,0:T(8,128)}, f32[48,8,2,512]{3,1,2,0:T(8,128)S(1)}, u32[]{:S(2)}) copy-start(f32[48,8,2,512]{3,1,2,0:T(8,128)S(1)} %copy.94) | copy-start | bytes 4718596
  155.6 40.8 %copy-start.40 = (f32[768]{0:T(1024)S(1)}, f32[768]{0:T(1024)}, u32[]{:S(2)}) copy-start(f32[768]{0:T(1024)} %param.38) | copy-start | bytes 9220
  155.6 45.4 %all-gather.11.cloned.1.call-start = ((), (), s32[]{:S(2)}) async-start(), calls=%async_computation.13 | async-start | bytes 2506752 | tf_op jit(solution)/shard_map/all_gather | solution.py:55
  156.2 71.2 %all-gather.9.cloned.1.call-start = ((), (), s32[]{:S(2)}) async-start(), calls=%async_computation.12 | async-start | bytes 2359296 | tf_op jit(solution)/shard_map/all_gather | solution.py:157
  200.2 72.3 %all-gather.13.cloned.1.call-start = ((), (), s32[]{:S(2)}) async-start(), calls=%async_computation.14 | async-start | bytes 2506752 | tf_op jit(solution)/shard_map/all_gather | solution.py:56
  200.8 121.7 %reduce-scatter.13.cloned.1.call-start = ((), (), s32[]{:S(2)}) async-start(), calls=%async_computation.15 | async-start | bytes 4718592 | tf_op jit(solution)/shard_map/reduce_scatter | solution.py:163
  279.4 43.1 %copy-start.42 = (f32[768]{0:T(1024)S(1)}, f32[768]{0:T(1024)}, u32[]{:S(2)}) copy-start(f32[768]{0:T(1024)} %param.40) | copy-start | bytes 9220
  279.4 79.8 %all-gather.15.cloned.1.call-start = ((), (), s32[]{:S(2)}) async-start(), calls=%async_computation.16 | async-start | bytes 2359296 | tf_op jit(solution)/shard_map/all_gather | solution.py:185
  329.1 89.9 %copy-start.33 = (f32[512]{0:T(512)}, f32[512]{0:T(512)S(1)}, u32[]{:S(2)}) copy-start(f32[512]{0:T(512)S(1)} %negate_multiply_fusion.2) | copy-start | bytes 6148
  332.0 87.1 %reduce-scatter.15.cloned.1.call-start = ((), (), s32[]{:S(2)}) async-start(), calls=%async_computation.17 | async-start | bytes 4718592 | tf_op jit(solution)/shard_map/reduce_scatter | solution.py:193
  359.2 12.2 %copy-start.61 = (bf16[1536,768]{1,0:T(8,128)(2,1)S(1)}, bf16[1536,768]{1,0:T(8,128)(2,1)}, u32[]{:S(2)}) copy-start(bf16[1536,768]{1,0:T(8,128)(2,1)} %all-gather.11.cloned.1.call-done) | copy-start | bytes 7077892
  375.7 77.6 %all-gather.17.cloned.1.call-start = ((), (), s32[]{:S(2)}) async-start(), calls=%async_computation.18 | async-start | bytes 2359296 | tf_op jit(solution)/shard_map/all_gather | solution.py:202
  426.0 129.4 %reduce-scatter.17.cloned.1.call-start = ((), (), s32[]{:S(2)}) async-start(), calls=%async_computation.19 | async-start | bytes 2359296 | tf_op jit(solution)/shard_map/reduce_scatter | solution.py:260
  481.0 5.9 copy-start
  481.0 5.9 copy-start.5
  505.8 5.9 copy-start
  505.8 5.9 copy-start.5
  513.5 4.1 copy-start.21
  522.3 106.6 %reduce-scatter.29.cloned.1.call-start = ((), (), s32[]{:S(2)}) async-start(), calls=%async_computation.25 | async-start | bytes 5013504 | tf_op jit(solution)/shard_map/reduce_scatter | solution.py:272
  530.4 178.1 %reduce-scatter.27.cloned.1.call-start = ((), (), s32[]{:S(2)}) async-start(), calls=%async_computation.24 | async-start | bytes 5013504 | tf_op jit(solution)/shard_map/reduce_scatter | solution.py:271
  538.6 231.8 %reduce-scatter.25.cloned.1.call-start = ((), (), s32[]{:S(2)}) async-start(), calls=%async_computation.23 | async-start | bytes 1253376 | tf_op jit(solution)/shard_map/reduce_scatter | solution.py:270
  542.3 289.3 %reduce-scatter.23.cloned.1.call-start = ((), (), s32[]{:S(2)}) async-start(), calls=%async_computation.22 | async-start | bytes 1253376 | tf_op jit(solution)/shard_map/reduce_scatter | solution.py:269
  546.0 346.7 %reduce-scatter.21.cloned.1.call-start = ((), (), s32[]{:S(2)}) async-start(), calls=%async_computation.21 | async-start | bytes 1253376 | tf_op jit(solution)/shard_map/reduce_scatter | solution.py:268
  548.0 4.5 copy-start.55
  548.0 4.8 copy-start.54
  548.0 5.1 copy-start.53
  548.0 406.1 %reduce-scatter.19.cloned.1.call-start = ((), (), s32[]{:S(2)}) async-start(), calls=%async_computation.20 | async-start | bytes 1253376 | tf_op jit(solution)/shard_map/reduce_scatter | solution.py:267
  548.3 7.1 copy-start.14
  551.7 3.8 copy-start.41
  551.7 3.8 copy-start.43
  551.7 3.8 copy-start.49
  555.5 5.2 copy-start.44
  555.5 5.2 copy-start.45
  555.5 5.1 copy-start.46
  555.5 5.1 copy-start.47
  555.5 5.1 copy-start.51
  555.5 5.1 copy-start.52
  (40 other events, 79.7 us)
Sparse Core Ops, SparseCore 0:
  10.4 27.5 all-gather.6
  155.7 40.5 reduce-scatter.10
  279.6 42.9 reduce-scatter.12
  426.1 27.1 all-gather.16
  522.4 26.0 reduce-scatter.16
  552.8 75.9 reduce-scatter.28
  633.8 74.6 reduce-scatter.26
  712.7 57.6 reduce-scatter.24
  774.6 57.0 reduce-scatter.22
  835.7 57.0 reduce-scatter.20
  897.0 57.0 reduce-scatter.18
Sparse Core Ops, SparseCore 1:
  158.6 39.7 all-gather.10
  200.5 26.8 all-gather.8
  229.8 42.7 all-gather.12
  332.1 27.1 all-gather.14
  375.8 43.2 reduce-scatter.14
where the time goes:
time: 976 us; the launch traced here: 963 us
  waiting for transfers between devices  537 us (55%)
  blocking collectives  169 us (17%)
  matrix products  129 us (13%)
  local copies, waits for them, and re-layouts  59 us (6%)
  other arithmetic  45.3 us (5%)
  between operations  22 us (2%)
    psum x2, blocking collectives, on_device(): lax.psum((jnp.sum(valid_own.astype(jnp.float32)), jnp.sum(masked * masked...  84.6 us
    reduce_scatter x1, waiting for transfers between devices, on_device(): lax.psum_scatter(grad_w_up, 'dp', scatter_dimension=0, tiled=True)  79.6 us
    reduce_scatter x1, waiting for transfers between devices, on_device(): lax.psum_scatter(grad_w_out, 'dp', scatter_dimension=0, tiled=True)  61.9 us
    reduce_scatter x1, waiting for transfers between devices, on_device(): lax.psum_scatter(grad_w_query, 'dp', scatter_dimension=0, tiled=True)  61.3 us
    reduce_scatter x1, waiting for transfers between devices, on_device(): lax.psum_scatter(grad_w_value, 'dp', scatter_dimension=0, tiled=True)  61.3 us
    reduce_scatter x1, waiting for transfers between devices, on_device(): lax.psum_scatter(grad_w_key, 'dp', scatter_dimension=0, tiled=True)  61.1 us
    reduce_scatter x1, waiting for transfers between devices, on_device(): lax.psum_scatter(times_plain(grad_upper, ffn_back[0]), 'tensor', scatter_...  43.3 us
    dot_general x6, matrix products, times_trans(): lax.dot_general(left, right, (((1,), (1,)), ((), ())), preferred_element_...  39.5 us
  transfers between devices with their start and end apart: 16, of which 13 were waited for; matrix products, arithmetic and copies ran while one was open for 6% of the time, Pallas kernels for 0%

commit v1 on v0

--- a/solution.py
+++ b/solution.py
@@ -1,8 +1,11 @@
+import functools
 import math
 
 import jax
 import jax.numpy as jnp
 from jax import lax
+from jax.experimental import pallas as pl
+from jax.experimental.pallas import tpu as pltpu
 from jax.sharding import PartitionSpec as P
 
 D = 768
@@ -317,9 +320,607 @@
     )
 
 
+MESH = pl.DeviceIdType.MESH
+F32 = jnp.float32
+BF16 = jnp.bfloat16
+
+
+def place():
+    dp = lax.axis_index("dp")
+    return dp // 4, (dp // 2) % 2, dp % 2, lax.axis_index("tensor")
+
+
+def device(z, x, c, y):
+    return ((z * 2 + x) * 2 + c, y)
+
+
+def shard_of(z, x, c, y):
+    return y * 16 + z * 4 + x * 2 + c
+
+
+def remote(src, dst, send_sem, recv_sem, to):
+    return pltpu.make_async_remote_copy(
+        src_ref=src,
+        dst_ref=dst,
+        send_sem=send_sem,
+        recv_sem=recv_sem,
+        device_id=to,
+        device_id_type=MESH,
+    )
+
+
+def greet(partners):
+    barrier = pltpu.get_barrier_semaphore()
+    for partner in partners:
+        pl.semaphore_signal(barrier, inc=1, device_id=partner, device_id_type=MESH)
+    pl.semaphore_wait(barrier, len(partners))
+
+
+class Around:
+    def __init__(self):
+        z, x, c, y = place()
+        self.z, self.x, self.c, self.y = z, x, c, y
+        self.first = (x ^ c, y ^ (1 - c))
+        self.second = (x ^ (1 - c), y ^ c)
+        self.both = (1 - x, 1 - y)
+        self.zs = [z ^ 1, z ^ 2, z ^ 3]
+        self.sibling = device(z, x, 1 - c, y)
+        self.by_first = device(z, self.first[0], c, self.first[1])
+        self.by_second = device(z, self.second[0], c, self.second[1])
+        self.by_z = [device(q, x, c, y) for q in self.zs]
+        self.by_x = device(z, 1 - x, c, y)
+        self.by_y = device(z, x, c, 1 - y)
+        self.across = device(z, x, 1 - c, 1 - y)
+        self.all = [self.sibling, self.by_first, self.by_second] + self.by_z + [self.across]
+
+
+def gather_kernel(
+    x_in, t_in, p1, p2, x_out, t_out, g1, g2, send1, send2, recv1, recv2, swap_s, swap_r, local
+):
+    d = Around()
+    z, x, c, y = d.z, d.x, d.c, d.y
+    greet(d.all)
+    me = shard_of(z, x, c, y)
+    swap_x = remote(x_in, x_out, swap_s.at[0], swap_r.at[0], d.across)
+    swap_t = remote(t_in, t_out, swap_s.at[1], swap_r.at[1], d.across)
+    keep_x = pltpu.make_async_copy(x_in, x_out, local.at[0])
+    keep_t = pltpu.make_async_copy(t_in, t_out, local.at[1])
+
+    @pl.when(c != y)
+    def _():
+        swap_x.start()
+
+    @pl.when(c == y)
+    def _():
+        keep_x.start()
+        keep_t.start()
+
+    pending = []
+
+    def group(own, full, send_sems, recv_sems, local_sem):
+        count = [0]
+
+        def send(src, shard, to):
+            copy = remote(src, full.at[shard], send_sems.at[count[0]], recv_sems.at[shard], to)
+            count[0] += 1
+            copy.start()
+            pending.append(copy)
+
+        def got(shard, source):
+            remote(
+                full.at[shard], full.at[shard], send_sems.at[0], recv_sems.at[shard], source
+            ).wait_recv()
+
+        keep = pltpu.make_async_copy(own, full.at[me], local_sem)
+        keep.start()
+        send(own, me, d.by_second)
+        send(own, me, d.by_first)
+        for to in d.by_z:
+            send(own, me, to)
+        send(own, me, d.sibling)
+
+        def from_first(q):
+            shard = shard_of(q, d.first[0], c, d.first[1])
+            got(shard, d.by_first)
+            send(full.at[shard], shard, d.by_second)
+            send(full.at[shard], shard, d.sibling)
+
+        from_first(z)
+        for q, source in zip(d.zs, d.by_z):
+            shard = shard_of(q, x, c, y)
+            got(shard, source)
+            send(full.at[shard], shard, d.by_second)
+            send(full.at[shard], shard, d.by_first)
+            send(full.at[shard], shard, d.sibling)
+        for q in d.zs:
+            from_first(q)
+        for xx, yy in (d.second, d.both):
+            for q in [z] + d.zs:
+                shard = shard_of(q, xx, c, yy)
+                got(shard, d.by_second)
+                send(full.at[shard], shard, d.sibling)
+
+        def finish():
+            keep.wait()
+            for q in [z] + d.zs:
+                for xx, yy in ((x, y), d.first, d.second, d.both):
+                    got(shard_of(q, xx, 1 - c, yy), d.sibling)
+
+        return finish
+
+    finish1 = group(p1, g1, send1, recv1, local.at[2])
+
+    @pl.when(c != y)
+    def _():
+        swap_t.start()
+
+    finish2 = group(p2, g2, send2, recv2, local.at[3])
+    finish1()
+    finish2()
+    for copy in pending:
+        copy.wait_send()
+
+    @pl.when(c != y)
+    def _():
+        swap_x.wait()
+        swap_t.wait()
+
+    @pl.when(c == y)
+    def _():
+        keep_x.wait()
+        keep_t.wait()
+
+
+def any_spec():
+    return pl.BlockSpec(memory_space=pl.ANY)
+
+
+def vmem_spec():
+    return pl.BlockSpec(memory_space=pltpu.VMEM)
+
+
+def shaped(shape, dtype):
+    return jax.ShapeDtypeStruct(shape, dtype)
+
+
+def dma(*shape):
+    return pltpu.SemaphoreType.DMA(shape)
+
+
+def gather_all(inputs, teacher, pack1, pack2):
+    return pl.pallas_call(
+        gather_kernel,
+        out_shape=(
+            shaped(inputs.shape, BF16),
+            shaped(teacher.shape, BF16),
+            shaped((32,) + pack1.shape, BF16),
+            shaped((32,) + pack2.shape, BF16),
+        ),
+        in_specs=[any_spec()] * 4,
+        out_specs=(any_spec(),) * 4,
+        scratch_shapes=[dma(31), dma(31), dma(32), dma(32), dma(2), dma(2), dma(4)],
+        compiler_params=pltpu.CompilerParams(collective_id=1, has_side_effects=True),
+        name="gather_all",
+    )(inputs, teacher, pack1, pack2)
+
+
+def sum_into(target, sources, rows, step=24):
+    def body(i, carry):
+        span = pl.ds(pl.multiple_of(i * step, step), step)
+        total = sources[0][span, :].astype(F32)
+        for source in sources[1:]:
+            total = total + source[span, :].astype(F32)
+        target[span, :] = total.astype(target.dtype)
+        return carry
+
+    lax.fori_loop(0, rows // step, body, 0)
+
+
+def scatter_kernel(
+    part_f, part_q, out_in, grad_in, vec,
+    sum_f, sum_q, out_swap, grad_swap, vec_sum,
+    b0_f, b1_f, b2_f, b3_f, b0_q, b1_q, b2_q, b3_q, va, vb,
+    s0_f, s1_f, s0_q, s1_q,
+    r0_f, r1_f, r2_f, r3_f, r0_q, r1_q, r2_q, r3_q,
+    vec_s, vec_r, swap_s, swap_r,
+):
+    d = Around()
+    z, x, c, y = d.z, d.x, d.c, d.y
+    greet(d.all)
+    swap_o = remote(out_in, out_swap, swap_s.at[0], swap_r.at[0], d.across)
+    swap_g = remote(grad_in, grad_swap, swap_s.at[1], swap_r.at[1], d.across)
+
+    @pl.when(c != y)
+    def _():
+        swap_o.start()
+        swap_g.start()
+
+    pending = []
+    order = d.zs + [z]
+
+    def slot(q, xy):
+        return q * 4 + xy[0] * 2 + xy[1]
+
+    def to_sibling(part, b0, send_sems, recv_sems):
+        count = 0
+        for xy in (d.both, d.first, d.second, (x, y)):
+            for q in order:
+                at = slot(q, xy)
+                copy = remote(
+                    part.at[shard_of(q, xy[0], 1 - c, xy[1])],
+                    b0.at[at],
+                    send_sems.at[count],
+                    recv_sems.at[at],
+                    d.sibling,
+                )
+                count += 1
+                copy.start()
+                pending.append(copy)
+
+    def got(buffer, at, sems, source):
+        remote(buffer.at[at], buffer.at[at], s0_f.at[0], sems.at[at], source).wait_recv()
+
+    to_sibling(part_f, b0_f, s0_f, r0_f)
+    to_sibling(part_q, b0_q, s0_q, r0_q)
+
+    def group(part, rows, b0, b1, b2, b3, send_sems, r0, r1, r2, r3, total):
+        count = [0]
+
+        def send(src, dst, sem, to):
+            copy = remote(src, dst, send_sems.at[count[0]], sem, to)
+            count[0] += 1
+            copy.start()
+            pending.append(copy)
+
+        for j, xy in enumerate((d.both, d.second)):
+            for q in order:
+                at = slot(q, xy)
+                got(b0, at, r0, d.sibling)
+                sum_into(b0.at[at], [b0.at[at], part.at[shard_of(q, xy[0], c, xy[1])]], rows)
+                send(b0.at[at], b1.at[j * 4 + q], r1.at[j * 4 + q], d.by_second)
+        for q in order:
+            at = slot(q, d.first)
+            got(b0, at, r0, d.sibling)
+            got(b1, q, r1, d.by_second)
+            own = part.at[shard_of(q, d.first[0], c, d.first[1])]
+            sum_into(b0.at[at], [b0.at[at], own, b1.at[q]], rows)
+            send(b0.at[at], b2.at[q], r2.at[q], d.by_first)
+        for i, q in enumerate(d.zs):
+            at = slot(q, (x, y))
+            got(b0, at, r0, d.sibling)
+            got(b1, 4 + q, r1, d.by_second)
+            got(b2, q, r2, d.by_first)
+            own = part.at[shard_of(q, x, c, y)]
+            sum_into(b0.at[at], [b0.at[at], own, b1.at[4 + q], b2.at[q]], rows)
+            send(b0.at[at], b3.at[i], r3.at[i], d.by_z[i])
+
+        def finish():
+            at = slot(z, (x, y))
+            got(b0, at, r0, d.sibling)
+            got(b1, 4 + z, r1, d.by_second)
+            got(b2, z, r2, d.by_first)
+            for i in range(3):
+                got(b3, i, r3, d.by_z[i])
+            own = part.at[shard_of(z, x, c, y)]
+            sum_into(
+                total,
+                [b0.at[at], own, b1.at[4 + z], b2.at[z], b3.at[0], b3.at[1], b3.at[2]],
+                rows,
+            )
+
+        return finish
+
+    finish_f = group(part_f, 216, b0_f, b1_f, b2_f, b3_f, s1_f, r0_f, r1_f, r2_f, r3_f, sum_f)
+    finish_q = group(part_q, 72, b0_q, b1_q, b2_q, b3_q, s1_q, r0_q, r1_q, r2_q, r3_q, sum_q)
+    va[0] = vec[...]
+    for k, to in enumerate((d.sibling, d.by_x, d.by_y, d.by_z[0], d.by_z[1])):
+        copy = remote(va.at[k], vb.at[k], vec_s.at[k], vec_r.at[k], to)
+        copy.start()
+        pending.append(copy)
+        copy.wait_recv()
+        if k < 4:
+            va[k + 1] = va[k] + vb[k]
+        else:
+            vec_sum[...] = va[k] + vb[k]
+    finish_f()
+    finish_q()
+    for copy in pending:
+        copy.wait_send()
+
+    @pl.when(c != y)
+    def _():
+        swap_o.wait()
+        swap_g.wait()
+
+
+def scatter_all(part_f, part_q, out_low, grad_low, vec):
+    def buffers(rows):
+        return [pltpu.VMEM((n, rows, D), BF16) for n in (16, 8, 4, 3)]
+
+    return pl.pallas_call(
+        scatter_kernel,
+        out_shape=(
+            shaped((216, D), F32),
+            shaped((72, D), F32),
+            shaped(out_low.shape, BF16),
+            shaped(grad_low.shape, BF16),
+            shaped(vec.shape, F32),
+        ),
+        in_specs=[vmem_spec(), vmem_spec(), any_spec(), any_spec(), vmem_spec()],
+        out_specs=(vmem_spec(), vmem_spec(), any_spec(), any_spec(), vmem_spec()),
+        scratch_shapes=buffers(216)
+        + buffers(72)
+        + [pltpu.VMEM((5,) + vec.shape, F32), pltpu.VMEM((5,) + vec.shape, F32)]
+        + [dma(16), dma(15), dma(16), dma(15)]
+        + [dma(16), dma(8), dma(4), dma(3), dma(16), dma(8), dma(4), dma(3)]
+        + [dma(5), dma(5), dma(2), dma(2)],
+        compiler_params=pltpu.CompilerParams(
+            collective_id=2, has_side_effects=True, vmem_limit_bytes=60 << 20
+        ),
+        name="scatter_all",
+    )(part_f, part_q, out_low, grad_low, vec)
+
+
+def pair_kernel(own, both, send_sem, recv_sem, local):
+    d = Around()
+    greet([d.sibling])
+    copy = remote(own, both.at[d.c], send_sem.at[0], recv_sem.at[0], d.sibling)
+    copy.start()
+    keep = pltpu.make_async_copy(own, both.at[d.c], local.at[0])
+    keep.start()
+    keep.wait()
+    copy.wait_send()
+    remote(own, both.at[1 - d.c], send_sem.at[0], recv_sem.at[0], d.sibling).wait_recv()
+
+
+def pair(own):
+    return pl.pallas_call(
+        pair_kernel,
+        out_shape=shaped((2,) + own.shape, own.dtype),
+        in_specs=[any_spec()],
+        out_specs=any_spec(),
+        scratch_shapes=[dma(1), dma(1), dma(1)],
+        compiler_params=pltpu.CompilerParams(collective_id=3, has_side_effects=True),
+        name="pair",
+    )(own)
+
+
+def trade_kernel(parts, other, send_sem, recv_sem):
+    d = Around()
+    greet([d.sibling])
+    copy = remote(parts.at[1 - d.c], other, send_sem.at[0], recv_sem.at[0], d.sibling)
+    copy.start()
+    copy.wait()
+
+
+def trade(parts):
+    return pl.pallas_call(
+        trade_kernel,
+        out_shape=shaped(parts.shape[1:], parts.dtype),
+        in_specs=[any_spec()],
+        out_specs=any_spec(),
+        scratch_shapes=[dma(1), dma(1)],
+        compiler_params=pltpu.CompilerParams(collective_id=4, has_side_effects=True),
+        name="trade",
+    )(parts)
+
+
+def by_chip(
+    inputs,
+    teacher,
+    lengths,
+    w_query,
+    w_key,
+    w_value,
+    w_out,
+    w_up,
+    w_down,
+    b_query,
+    b_value,
+    b_out,
+    b_up,
+    b_down,
+    gain_one,
+    shift_one,
+    gain_two,
+    shift_two,
+    z_head,
+    z_mha,
+    z_hidden,
+    z_int,
+    z_ffn,
+):
+    z, x, core, y = place()
+    rows = inputs.shape[0]
+    head_size = D // HEADS
+    softmax_scale = 1.0 / math.sqrt(head_size)
+    halves = jnp.concatenate([lengths // 32, lengths % 32]).astype(BF16)
+    marks = jnp.pad(halves[None, :], ((0, 7), (0, D - 2)))
+    pack1 = jnp.concatenate([w_query, w_key, w_value, marks], axis=0)
+    pack2 = jnp.concatenate([w_up, w_down, w_out], axis=0)
+    source, target, full1, full2 = gather_all(inputs, teacher, pack1, pack2)
+    wq = full1[:, 0:24].reshape(D, D)
+    wk = full1[:, 24:48].reshape(D, D)
+    wv = full1[:, 48:72].reshape(D, D)
+    wu = full2[:, 0:96].reshape(FF, D)
+    wd = full2[:, 96:192].reshape(FF, D)
+    wo = full2[:, 192:216].reshape(D, D)
+    marks_all = full1[:16, 72, 0:2].astype(F32)
+    lengths_all = marks_all[:, 0] * 32.0 + marks_all[:, 1]
+    valid_count = jnp.sum(lengths_all)
+    length = lengths_all[z * 4 + x * 2 + y]
+    valid_keys = jnp.arange(SEQ, dtype=jnp.int32).astype(F32) < length
+    positions = core * rows + jnp.arange(rows, dtype=jnp.int32)
+    valid_own = positions.astype(F32) < length
+
+    query = ((times_trans(source, wq) + b_query) * softmax_scale).astype(BF16)
+    keys_own = times_trans(source, wk).astype(BF16)
+    values_own = (times_trans(source, wv) + b_value).astype(BF16)
+    kv = pair(jnp.concatenate([keys_own, values_own], axis=1)).reshape(SEQ, 2 * D)
+    query3 = query.reshape(rows, HEADS, head_size)
+    keys3 = kv[:, :D].reshape(SEQ, HEADS, head_size)
+    values3 = kv[:, D:].reshape(SEQ, HEADS, head_size)
+    scores = jnp.einsum("qhd,khd->hqk", query3, keys3, preferred_element_type=F32)
+    scores = jnp.where(valid_keys[None, None, :], scores, -1e30)
+    highest = jnp.max(scores, axis=-1, keepdims=True)
+    exponent = jnp.exp(scores - highest)
+    denominator = jnp.sum(exponent, axis=-1, keepdims=True)
+    attention = exponent / denominator
+    attention_b = attention.astype(BF16)
+    context_f = jnp.einsum("hqk,khd->qhd", attention_b, values3, preferred_element_type=F32)
+    gated = (context_f * z_head[None, :, None]).reshape(rows, D).astype(BF16)
+
+    attn_out = times_plain(gated, wo) + b_out
+    branch_attn = z_mha * z_hidden
+    first_sum = source.astype(F32) + branch_attn * attn_out
+    first_norm = norm_rows(first_sum, gain_one, shift_one)
+    first_low = first_norm.astype(BF16)
+    upper = times_trans(first_low, wu) + b_up
+    activated = gelu_exact(upper)
+    hidden_b = (activated * z_int).astype(BF16)
+    down = times_plain(hidden_b, wd) + b_down
+    branch_ffn = z_ffn * z_hidden
+    second_sum = first_norm + branch_ffn * down
+    output = norm_rows(second_sum, gain_two, shift_two)
+    residue = output - target.astype(F32)
+    masked = jnp.where(valid_own[:, None], residue, 0.0)
+    square_sum = jnp.sum(masked * masked)
+    tokens_all = rows * 32
+    grad_out = masked * (2.0 * tokens_all / valid_count)
+    unused, pull_two = jax.vjp(norm_rows, second_sum, gain_two, shift_two)
+    grad_second, grad_gain_two, grad_shift_two = pull_two(grad_out)
+    grad_down = (grad_second * branch_ffn).astype(BF16)
+    grad_z_ffn = jnp.sum(grad_second * z_hidden * down).reshape(1)
+    hidden_part = jnp.sum(grad_second * z_ffn * down, axis=0)
+    grad_b_down = jnp.sum(grad_down.astype(F32), axis=0)
+    grad_w_down = trans_times(hidden_b, grad_down).astype(BF16)
+    grad_hidden = times_trans(grad_down, wd)
+    grad_z_int = jnp.sum(grad_hidden * activated, axis=0)
+    unused, gelu_pull = jax.vjp(gelu_exact, upper)
+    grad_upper = gelu_pull(grad_hidden * z_int)[0].astype(BF16)
+    grad_b_up = jnp.sum(grad_upper.astype(F32), axis=0)
+    grad_w_up = trans_times(grad_upper, first_low).astype(BF16)
+    grad_first_norm = grad_second + times_plain(grad_upper, wu)
+    unused, pull_one = jax.vjp(norm_rows, first_sum, gain_one, shift_one)
+    grad_first, grad_gain_one, grad_shift_one = pull_one(grad_first_norm)
+    grad_attn = (grad_first * branch_attn).astype(BF16)
+    grad_z_mha = jnp.sum(grad_first * z_hidden * attn_out).reshape(1)
+    hidden_part = hidden_part + jnp.sum(grad_first * z_mha * attn_out, axis=0)
+    grad_b_out = jnp.sum(grad_attn.astype(F32), axis=0)
+    grad_w_out = trans_times(gated, grad_attn).astype(BF16)
+    grad_gated = times_trans(grad_attn, wo).reshape(rows, HEADS, head_size)
+    grad_z_head = jnp.sum(grad_gated * context_f, axis=(0, 2))
+    grad_heads = (grad_gated * z_head[None, :, None]).astype(BF16)
+
+    grad_attention = jnp.einsum(
+        "qhd,khd->hqk", grad_heads, values3, preferred_element_type=F32
+    )
+    row_dots = jnp.sum(attention * grad_attention, axis=-1, keepdims=True)
+    grad_scores = (attention * (grad_attention - row_dots)).astype(BF16)
+    grad_query = (
+        softmax_scale
+        * jnp.einsum("hqk,khd->qhd", grad_scores, keys3, preferred_element_type=F32)
+    ).astype(BF16).reshape(rows, D)
+    grad_keys_part = jnp.einsum(
+        "hqk,qhd->khd", grad_scores, query3, preferred_element_type=F32
+    ).reshape(2, rows, D)
+    grad_values_part = jnp.einsum(
+        "hqk,qhd->khd", attention_b, grad_heads, preferred_element_type=F32
+    ).reshape(2, rows, D)
+    parts = jnp.concatenate([grad_keys_part, grad_values_part], axis=2)
+    own_parts = lax.dynamic_index_in_dim(parts, core, 0, keepdims=False)
+    grad_kv = (own_parts + trade(parts)).astype(BF16)
+    grad_keys, grad_values = grad_kv[:, :D], grad_kv[:, D:]
+    grad_w_query = trans_times(grad_query, source).astype(BF16)
+    grad_w_key = trans_times(grad_keys, source).astype(BF16)
+    grad_w_value = trans_times(grad_values, source).astype(BF16)
+    grad_b_query = jnp.sum(grad_query.astype(F32), axis=0)
+    grad_b_value = jnp.sum(grad_values.astype(F32), axis=0)
+    grad_inputs = (
+        grad_first
+        + times_plain(grad_query, wq)
+        + times_plain(grad_keys, wk)
+        + times_plain(grad_values, wv)
+    )
+    part_f = jnp.concatenate(
+        [
+            grad_w_up.reshape(32, 96, D),
+            grad_w_down.reshape(32, 96, D),
+            grad_w_out.reshape(32, 24, D),
+        ],
+        axis=1,
+    )
+    part_q = jnp.concatenate(
+        [
+            grad_w_query.reshape(32, 24, D),
+            grad_w_key.reshape(32, 24, D),
+            grad_w_value.reshape(32, 24, D),
+        ],
+        axis=1,
+    )
+    pieces = (
+        grad_b_query,
+        grad_b_value,
+        grad_b_out,
+        grad_b_down,
+        grad_gain_one,
+        grad_shift_one,
+        grad_gain_two,
+        grad_shift_two,
+        hidden_part,
+        grad_b_up,
+        grad_z_int,
+        grad_z_head,
+        grad_z_mha,
+        grad_z_ffn,
+        square_sum.reshape(1),
+    )
+    flat = jnp.concatenate(pieces)
+    vec = jnp.pad(flat, (0, 104 * 128 - flat.shape[0])).reshape(104, 128)
+    sum_f, sum_q, out_swap, grad_swap, vec_sum = scatter_all(
+        part_f, part_q, output.astype(BF16), grad_inputs.astype(BF16), vec
+    )
+    total = vec_sum.reshape(-1)
+    sums = []
+    at = 0
+    for piece in pieces:
+        sums.append(total[at : at + piece.shape[0]])
+        at += piece.shape[0]
+    home = core == y
+    layer_out = jnp.where(home, output, out_swap.astype(F32))
+    grad_home = jnp.where(home, grad_inputs, grad_swap.astype(F32))
+    (s_bq, s_bv, s_bo, s_bd, s_g1, s_s1, s_g2, s_s2, s_zh, s_bu, s_zi, s_hd, s_zm, s_zf, s_sq) = sums
+    return (
+        layer_out,
+        s_sq / (D * valid_count),
+        grad_home,
+        sum_q[0:24],
+        sum_q[24:48],
+        sum_q[48:72],
+        sum_f[192:216],
+        sum_f[0:96],
+        sum_f[96:192],
+        s_bq,
+        s_bv,
+        s_bo,
+        s_bu,
+        s_bd,
+        s_g1,
+        s_s1,
+        s_g2,
+        s_s2,
+        s_hd,
+        s_zm,
+        s_zh,
+        s_zi,
+        s_zf,
+    )
+
+
 def solution(mesh):
+    sizes = (mesh.shape["dp"], mesh.shape["tensor"])
     return jax.shard_map(
-        on_device,
+        by_chip if sizes == (16, 2) else on_device,
         mesh=mesh,
         in_specs=(
             P(("dp", "tensor"), None),

time: 976 us -> 492 us (0.50)
  waiting for transfers between devices: 537 us -> 0 us
  Pallas kernels: 0 us -> 246 us
  blocking collectives: 169 us -> 0 us
  between operations: 22 us -> 6.97 us
    reduce_scatter x10 -> x0, waiting for transfers between devices: 431 us -> none  [the longest x1 79.6 us: on_device(): lax.psum_scatter(grad_w_up, 'dp', scatter_dimension=0, tiled=True)]
    pallas_call x0 -> x4, Pallas kernels: none -> 246 us  [the longest x1 100 us: scatter_all(): pl.pallas_call(scatter_kernel, out_shape=(shaped((216, D), F32), shaped((...]
    all_gather x6 -> x0, waiting for transfers between devices: 104 us -> none  [the longest x1 27.2 us: on_device(): down_group = lax.all_gather(grad_down, 'tensor', axis=0, tiled=True)]
    psum x2 -> x0, blocking collectives: 84.6 us -> none  [on_device(): lax.psum((jnp.sum(valid_own.astype(jnp.float32)), jnp.sum(masked * masked...]
    all_gather x4 -> x0, blocking collectives: 84 us -> none  [the longest x1 23.3 us: gather_attn(): lax.all_gather(w_key, 'dp', axis=0, tiled=True)]
    dynamic_update_slice x9 -> x0, local copies, waits for them, and re-layouts: 32.9 us -> none  [the longest x4 31.6 us: forward_seq(): return lax.map(forward_block, query_seq)]
    reduce_sum x13 -> x5, other arithmetic: 28.1 us -> 5.86 us  [the longest x1 3.04 us: by_chip(): square_sum = jnp.sum(masked * masked)]
    slice x0 -> x13, local copies, waits for them, and re-layouts: none -> 22.1 us  [the longest x1 6.84 us: by_chip(): wd = full2[:, 96:192].reshape(FF, D)]
  transfers between devices with their start and end apart: 16 -> 0, of which waited for: 13 -> 0; matrix products, arithmetic and copies ran while one was open for 6% -> 0% of each run, Pallas kernels for 0% -> 0%
where the time goes in v1:
time: 492 us; the launch traced here: 485 us
  Pallas kernels  246 us (50%)
  matrix products  127 us (26%)
  local copies, waits for them, and re-layouts  54.3 us (11%)
  other arithmetic  50.9 us (10%)
  between operations  6.97 us (1%)
    pallas_call x1, Pallas kernels, scatter_all(): pl.pallas_call(scatter_kernel, out_shape=(shaped((216, D), F32), shaped((...  100 us
    pallas_call x1, Pallas kernels, gather_all(): pl.pallas_call(gather_kernel, out_shape=(shaped(inputs.shape, BF16), shap...  90.3 us
    pallas_call x1, Pallas kernels, pair(): pl.pallas_call(pair_kernel, out_shape=shaped((2,) + own.shape, own.dtype)...  49.2 us
    dot_general x6, matrix products, times_trans(): lax.dot_general(left, right, (((1,), (1,)), ((), ())), preferred_element_...  33.8 us
    dot_general x1, matrix products, by_chip(): jnp.einsum('qhd,khd->hqk', grad_heads, values3, preferred_element_type=F32)  19.3 us
    convert_element_type x1, other arithmetic, by_chip(): grad_scores = (attention * (grad_attention - row_dots)).astype(BF16)  16.3 us
    sub x1, matrix products, by_chip(): exponent = jnp.exp(scores - highest)  12.8 us
    dot_general x6, matrix products, times_plain(): return jnp.dot(left, right, preferred_element_type=jnp.float32)  12.3 us

profile of v1, /device:TPU:6, one launch (start us, length us, event | category | flops | bytes accessed | tf_op | source)
XLA Modules:
  0.0 485.5 jit_solution(6374376792081683042)
XLA Ops:
  1.4 1.5 pad_maximum_fusion.5.p1
  2.9 1.8 pad_maximum_fusion.4.p2
  4.6 90.3 %gather_all.1 = (bf16[512,768]{1,0:T(8,128)(2,1)}, bf16[512,768]{1,0:T(8,128)(2,1)}, bf16[32,80,768]{2,1,0:T(8,128)(2,1)}, bf16[32,216,768]{2,1,0:T(8,128)(2,1)}) custom-call(bf16[512,768]{1,0:T(8,128)(2,1)} %x_in.1, bf16[512,768]{1,0:T(8,128)(2,1)} %t_in.1, bf16[80,768]{1,0:T(8,128)(2,1)} %pad_maximum_fusion.5.p1, bf16[216,768]{1,0:T(8,128)(2,1)} %pad_maximum_fusion.4.p2), custom_call_target="tpu_custom_call" | custom-call | tf_op jit(solution)/shard_map/gather_all/pallas_call | solution.py:491
  94.9 2.3 fusion.56
  97.3 1.0 copy-done.28
  99.1 1.2 copy.61
  100.2 2.0 convolution_convert_fusion.6
  103.1 1.3 pad_maximum_fusion.3.own
  104.4 49.2 %pair.1 = bf16[2,512,1536]{2,1,0:T(8,128)(2,1)} custom-call(bf16[512,1536]{1,0:T(8,128)(2,1)} %pad_maximum_fusion.3.own), custom_call_target="tpu_custom_call" | custom-call | tf_op jit(solution)/shard_map/pair/pallas_call | solution.py:677
  153.6 3.2 fusion.57
  156.8 2.0 copy.62
  161.6 12.8 %fusion.61 = (f32[12,512]{1,0:T(8,128)S(1)}, f32[12,512,1024]{2,1,0:T(8,128)}) fusion(pred[1024]{0:T(1024)(128)(4,1)S(1)} %convert_compare_fusion, bf16[512,12,64]{0,2,1:T(8,128)(2,1)} %bitcast.141, bf16[1024,12,64]{0,2,1:T(8,128)(2,1)S(1)} %bitcast.129), kind=kOutput, calls=%fused_computation.154 | convolution fusion | flops 824181760 | bytes 27550720 | tf_op jit(solution)/shard_map/sub | solution.py:766
  175.2 12.0 %fusion.23 = (bf16[512,12,64]{0,2,1:T(8,128)(2,1)S(1)}, f32[12,64,512]{2,1,0:T(8,128)}) fusion(f32[12]{0:T(128)S(1)} %copy-done.59, bf16[1024,12,64]{0,2,1:T(8,128)(2,1)S(1)} %bitcast.143, f32[12,512,1024]{2,1,0:T(8,128)} %get-tuple-element.105, f32[12,512]{1,0:T(8,128)S(1)} %get-tuple-element.104), kind=kOutput, calls=%fused_computation.51 | convolution fusion | flops 818675712 | bytes 29122608 | tf_op jit(solution)/shard_map/hqk,khd->qhd/dot_general | solution.py:770
  187.2 1.7 slice.143
  190.2 2.0 fusion.54
  192.6 6.8 %fusion.55 = (bf16[32,96,768]{2,1,0:T(8,128)(2,1)}, bf16[32,96,768]{2,1,0:T(8,128)(2,1)S(1)}) fusion(bf16[32,216,768]{2,1,0:T(8,128)(2,1)} %get-tuple-element.34), kind=kLoop, calls=%fused_computation.148 | loop fusion | bytes 18874368 | tf_op jit(solution)/shard_map/slice | solution.py:746
  199.5 20.2 %multiply_convert_fusion.1 = (bf16[512,3072]{1,0:T(8,128)(2,1)S(1)}, f32[512,3072]{1,0:T(8,128)}, f32[512,3072]{1,0:T(8,128)}) fusion(f32[3072]{0:T(1024)S(1)} %copy-done.53, f32[3072]{0:T(1024)S(1)} %copy-done.54, bf16[3072,768]{1,0:T(8,128)(2,1)S(1)} %bitcast.133, f32[512,768]{1,0:T(8,128)S(1)} %get-tuple-element.71, f32[768]{0:T(1024)S(1)} %copy-done.58, ...), kind=kOutput, calls=%fused_computation.18 | convolution fusion | flops 2523267072 | bytes 22054912 | tf_op jit(solution)/shard_map/dot_general | solution.py:36
  219.8 3.9 fusion.52
  225.5 3.0 multiply_reduce_fusion.2
  228.6 2.1 fusion.50
  231.2 9.0 %convert_reduce_fusion = (f32[3072]{0:T(1024)S(1)}, bf16[512,3072]{1,0:T(8,128)(2,1)S(1)}, f32[3072]{0:T(1024)S(1)}) fusion(f32[512,3072]{1,0:T(8,128)} %get-tuple-element.69, f32[3072]{0:T(1024)S(1)} %copy-done.53, f32[512,3072]{1,0:T(8,128)} %get-tuple-element.109, f32[3072]{0:T(1024)S(1)} %copy-done.54, bf16[512,768]{1,0:T(8,128)(2,1)S(1)} %get-tuple-element.57, ...), kind=kOutput, calls=%fused_computation.16 | convolution fusion | flops 2448943104 | bytes 21282816 | tf_op jit(solution)/shard_map/dot_general | solution.py:36
  240.3 3.0 multiply_reduce_fusion.8
  244.7 1.0 copy-done.25
  245.8 1.8 multiply_reduce_fusion.3
  249.3 19.3 %multiply_reduce_fusion = (f32[12,512]{1,0:T(8,128)S(1)}, f32[12,512,1024]{2,1,0:T(8,128)}) fusion(f32[12,512,1024]{2,1,0:T(8,128)} %get-tuple-element.105, f32[12,512]{1,0:T(8,128)S(1)} %get-tuple-element.104, bf16[1024,12,64]{0,2,1:T(8,128)(2,1)S(1)} %bitcast.144, f32[512,12,64]{0,2,1:T(8,128)S(1)} %get-tuple-element.119, f32[12]{0:T(128)S(1)} %copy-done.59), kind=kOutput, calls=%fused_computation.2 | convolution fusion | flops 824961024 | bytes 53526576 | tf_op jit(solution)/shard_map/qhd,khd->hqk/dot_general | solution.py:815
  268.7 16.3 %multiply_convert_fusion = bf16[12,512,1024]{2,1,0:T(8,128)(2,1)S(1)} fusion(f32[12,512,1024]{2,1,0:T(8,128)} %get-tuple-element.113, f32[12,512]{1,0:T(8,128)S(1)} %get-tuple-element.112, f32[12,512,1024]{2,1,0:T(8,128)} %get-tuple-element.105, f32[12,512]{1,0:T(8,128)S(1)} %get-tuple-element.104), kind=kLoop, calls=%fused_computation.1 | loop fusion | flops 25165824 | bytes 62963712 | tf_op jit(solution)/shard_map/convert_element_type | solution.py:819
  284.9 7.4 %convert_reduce_fusion.4 = (f32[12,64]{1,0:T(8,128)S(1)}, bf16[12,64,512]{2,1,0:T(8,128)(2,1)}) fusion(bf16[1024,12,64]{0,2,1:T(8,128)(2,1)} %bitcast.130, bf16[12,512,1024]{2,1,0:T(8,128)(2,1)S(1)} %multiply_convert_fusion), kind=kOutput, calls=%fused_computation.65 | convolution fusion | flops 806878464 | bytes 14945280 | tf_op jit(solution)/shard_map/hqk,khd->qhd/dot_general | solution.py:822
  292.4 7.1 %convolution_bitcast_fusion = f32[1024,12,64]{0,2,1:T(8,128)S(1)} fusion(bf16[512,12,64]{0,2,1:T(8,128)(2,1)} %bitcast.142, bf16[12,512,1024]{2,1,0:T(8,128)(2,1)} %copy-done), kind=kOutput, calls=%fused_computation.46 | convolution fusion | flops 805306368 | bytes 16515072 | tf_op jit(solution)/shard_map/hqk,qhd->khd/dot_general | solution.py:824
  299.5 4.1 reshape.283
  303.6 4.0 copy.63
  307.6 11.7 %fusion.20 = f32[1024,12,64]{0,2,1:T(8,128)} fusion(f32[512,12,64]{0,2,1:T(8,128)} %copy-done.22, f32[12]{0:T(128)S(1)} %copy-done.59, f32[12,512,1024]{2,1,0:T(8,128)} %get-tuple-element.105, f32[12,512]{1,0:T(8,128)S(1)} %get-tuple-element.104), kind=kOutput, calls=%fused_computation.47 | convolution fusion | flops 818675712 | bytes 29909040 | tf_op jit(solution)/shard_map/hqk,qhd->khd/dot_general | solution.py:827
  319.4 5.6 %reshape.284 = f32[2,512,768]{1,0,2:T(2,128)} reshape(f32[1024,12,64]{0,2,1:T(8,128)} %fusion.20) | data formatting | bytes 6291456 | tf_op jit(solution)/shard_map/reshape | solution.py:829
  325.0 5.9 %copy.64 = f32[2,512,768]{2,1,0:T(8,128)} copy(f32[2,512,768]{1,0,2:T(2,128)} %reshape.284) | data formatting | bytes 6291456 | tf_op jit(solution)/shard_map/reshape | solution.py:829
  330.9 5.3 %pad_maximum_fusion.1.parts = f32[2,512,1536]{2,1,0:T(8,128)} fusion(f32[2,512,768]{2,1,0:T(8,128)} %copy.64, f32[2,512,768]{2,1,0:T(8,128)S(1)} %copy.63), kind=kLoop, calls=%fused_computation.12 | loop fusion | flops 1572864 | bytes 12582912 | tf_op jit(solution)/shard_map/concatenate | solution.py:830
  336.1 6.0 %trade.1 = f32[512,1536]{1,0:T(8,128)} custom-call(f32[2,512,1536]{2,1,0:T(8,128)} %pad_maximum_fusion.1.parts), custom_call_target="tpu_custom_call" | custom-call | tf_op jit(solution)/shard_map/trade/pallas_call | solution.py:697
  342.1 2.7 fusion.19
  344.9 1.1 copy-done.11
  346.2 2.0 concatenate.45
  348.8 2.3 convolution_convert_fusion.4
  352.8 2.0 pad_maximum_fusion.2.part_q
  354.9 1.5 copy-done.63
  356.4 3.3 convolution_convert_fusion.1
  359.8 2.9 convolution_convert_fusion
  363.5 5.2 %pad_maximum_fusion.part_f = bf16[32,216,768]{2,1,0:T(8,128)(2,1)} fusion(bf16[32,24,768]{2,1,0:T(8,128)(2,1)S(1)} %bitcast.152, bf16[32,96,768]{2,1,0:T(8,128)(2,1)S(1)} %bitcast.140, bf16[32,96,768]{2,1,0:T(8,128)(2,1)S(1)} %bitcast.139), kind=kLoop, calls=%fused_computation.9 | loop fusion | flops 31850496 | bytes 21233664 | tf_op jit(solution)/shard_map/concatenate | solution.py:845
  371.7 1.7 fusion.62
  373.5 100.3 %scatter_all.1 = (f32[216,768]{1,0:T(8,128)}, f32[72,768]{1,0:T(8,128)}, bf16[512,768]{1,0:T(8,128)(2,1)}, bf16[512,768]{1,0:T(8,128)(2,1)}, f32[104,128]{1,0:T(8,128)}) custom-call(bf16[32,216,768]{2,1,0:T(8,128)(2,1)} %pad_maximum_fusion.part_f, bf16[32,72,768]{2,1,0:T(8,128)(2,1)} %pad_maximum_fusion.2.part_q, bf16[512,768]{1,0:T(8,128)(2,1)} %get-tuple-element.80.out_in, ...), custom_call_target="tpu_custom_call" | custom-call | tf_op jit(solution)/shard_map/scatter_all/pallas_call | solution.py:640
  473.9 1.4 fusion.60
  476.6 3.5 convert_select_fusion
  (168 shorter events, 20.5 us)
Async XLA Ops:
  94.9 3.3 copy-start.33
  94.9 3.3 copy-start.55
  97.3 3.0 copy-start.26
  97.3 5.0 %copy-start.13 = (bf16[32,24,768]{2,1,0:T(8,128)(2,1)}, bf16[32,24,768]{2,1,0:T(8,128)(2,1)S(1)}, u32[]{:S(2)}) copy-start(bf16[32,24,768]{2,1,0:T(8,128)(2,1)S(1)} %get-tuple-element.76) | copy-start | bytes 3538948
  158.8 15.6 %copy-start.9 = (bf16[1024,768]{0,1:T(8,128)(2,1)}, bf16[1024,768]{0,1:T(8,128)(2,1)S(1)}, u32[]{:S(2)}) copy-start(bf16[1024,768]{0,1:T(8,128)(2,1)S(1)} %copy.62) | copy-start | bytes 4718596
  175.2 12.0 %copy-start.23 = (bf16[1024,768]{0,1:T(8,128)(2,1)}, bf16[1024,768]{0,1:T(8,128)(2,1)S(1)}, u32[]{:S(2)}) copy-start(bf16[1024,768]{0,1:T(8,128)(2,1)S(1)} %copy.59) | copy-start | bytes 4718596
  187.2 5.1 %copy-start.37 = (bf16[512,12,64]{0,2,1:T(8,128)(2,1)}, bf16[512,12,64]{0,2,1:T(8,128)(2,1)S(1)}, u32[]{:S(2)}) copy-start(bf16[512,12,64]{0,2,1:T(8,128)(2,1)S(1)} %get-tuple-element.106) | copy-start | bytes 2359300
  187.2 3.0 copy-start.50
  187.2 3.0 copy-start.35
  187.2 3.0 copy-start.51
  188.9 3.4 copy-start.7
  192.3 51.1 %copy-start.5 = (f32[512,768]{1,0:T(8,128)}, f32[512,768]{1,0:T(8,128)S(1)}, u32[]{:S(2)}) copy-start(f32[512,768]{1,0:T(8,128)S(1)} %get-tuple-element.71) | copy-start | bytes 4718596
  192.6 6.9 %copy-start.52 = (f32[768]{0:T(1024)S(1)}, f32[768]{0:T(1024)}, u32[]{:S(2)}) copy-start(f32[768]{0:T(1024)} %param.37) | copy-start | bytes 9220
  192.6 6.9 %copy-start.53 = (f32[3072]{0:T(1024)S(1)}, f32[3072]{0:T(1024)}, u32[]{:S(2)}) copy-start(f32[3072]{0:T(1024)} %param.44) | copy-start | bytes 36868
  192.6 6.9 %copy-start.54 = (f32[3072]{0:T(1024)S(1)}, f32[3072]{0:T(1024)}, u32[]{:S(2)}) copy-start(f32[3072]{0:T(1024)} %param.35) | copy-start | bytes 36868
  192.6 6.9 %copy-start.58 = (f32[768]{0:T(1024)S(1)}, f32[768]{0:T(1024)}, u32[]{:S(2)}) copy-start(f32[768]{0:T(1024)} %param.38) | copy-start | bytes 9220
  199.5 20.3 %copy-start.15 = (bf16[32,96,768]{2,1,0:T(8,128)(2,1)}, bf16[32,96,768]{2,1,0:T(8,128)(2,1)S(1)}, u32[]{:S(2)}) copy-start(bf16[32,96,768]{2,1,0:T(8,128)(2,1)S(1)} %get-tuple-element.74) | copy-start | bytes 14155780
  199.5 20.2 %copy-start.16 = (bf16[32,96,768]{2,1,0:T(8,128)(2,1)S(1)}, bf16[32,96,768]{2,1,0:T(8,128)(2,1)}, u32[]{:S(2)}) copy-start(bf16[32,96,768]{2,1,0:T(8,128)(2,1)} %get-tuple-element.73) | copy-start | bytes 14155780
  199.5 20.2 %copy-start.57 = (f32[768]{0:T(1024)S(1)}, f32[768]{0:T(1024)}, u32[]{:S(2)}) copy-start(f32[768]{0:T(1024)} %param.36) | copy-start | bytes 9220
  219.8 4.0 copy-start.60
  223.7 4.8 copy-start.1
  223.8 4.8 copy-start.42
  224.1 6.7 %copy-start.48 = (f32[512]{0:T(512)}, f32[512]{0:T(512)S(1)}, u32[]{:S(2)}) copy-start(f32[512]{0:T(512)S(1)} %fusion.43) | copy-start | bytes 6148
  225.5 3.1 copy-start.20
  228.6 2.6 copy-start.17
  230.7 9.6 %slice-start = ((s8[4718592]{0:T(1024)(128)(4,1)}), s8[4194304]{0:T(1024)(128)(4,1)S(1)}, s32[]{:S(2)}) async-start(s8[4718592]{0:T(1024)(128)(4,1)} %bitcast.134), calls=%async_computation | async-start | bytes 8388608
  231.0 9.3 %copy-start.31 = (bf16[512,768]{1,0:T(8,128)(2,1)}, bf16[512,768]{1,0:T(8,128)(2,1)S(1)}, u32[]{:S(2)}) copy-start(bf16[512,768]{1,0:T(8,128)(2,1)S(1)} %get-tuple-element.57) | copy-start | bytes 2359300
  231.2 9.1 %slice-start.1 = ((s8[4718592]{0:T(1024)(128)(4,1)}), s8[524288]{0:T(1024)(128)(4,1)S(1)}, s32[]{:S(2)}) async-start(s8[4718592]{0:T(1024)(128)(4,1)} %bitcast.134), calls=%async_computation.1 | async-start | bytes 1048576
  240.3 3.0 copy-start.62
  243.3 2.4 copy-start.25
  244.0 3.6 copy-start.3
  248.6 20.1 %copy-start.22 = (f32[512,12,64]{0,2,1:T(8,128)}, f32[512,12,64]{0,2,1:T(8,128)S(1)}, u32[]{:S(2)}) copy-start(f32[512,12,64]{0,2,1:T(8,128)S(1)} %get-tuple-element.119) | copy-start | bytes 4718596
  284.9 7.4 %copy-start = (bf16[12,512,1024]{2,1,0:T(8,128)(2,1)}, bf16[12,512,1024]{2,1,0:T(8,128)(2,1)S(1)}, u32[]{:S(2)}) copy-start(bf16[12,512,1024]{2,1,0:T(8,128)(2,1)S(1)} %multiply_convert_fusion) | copy-start | bytes 37748740
  348.8 2.3 copy-start.36
  352.8 3.6 copy-start.63
  356.4 3.3 copy-start.32
  356.4 3.3 copy-start.61
  359.7 3.0 copy-start.19
  359.8 3.0 copy-start.38
  363.5 5.2 %copy-start.29 = (bf16[32,24,768]{2,1,0:T(8,128)(2,1)S(1)}, bf16[32,24,768]{2,1,0:T(8,128)(2,1)}, u32[]{:S(2)}) copy-start(bf16[32,24,768]{2,1,0:T(8,128)(2,1)} %copy-done.28) | copy-start | bytes 3538948
  363.5 5.2 %copy-start.30 = (bf16[12,64,512]{2,1,0:T(8,128)(2,1)S(1)}, bf16[12,64,512]{2,1,0:T(8,128)(2,1)}, u32[]{:S(2)}) copy-start(bf16[12,64,512]{2,1,0:T(8,128)(2,1)} %get-tuple-element.117) | copy-start | bytes 2359300
  373.5 103.1 %copy-start.2 = (f32[512,768]{1,0:T(8,128)S(1)}, f32[512,768]{1,0:T(8,128)}, u32[]{:S(2)}) copy-start(f32[512,768]{1,0:T(8,128)} %copy-done.1) | copy-start | bytes 4718596
  373.5 103.1 %copy-start.43 = (f32[512]{0:T(512)S(1)}, f32[512]{0:T(512)}, u32[]{:S(2)}) copy-start(f32[512]{0:T(512)} %copy-done.42) | copy-start | bytes 6148
  373.5 103.1 %copy-start.45 = (f32[768]{0:T(1024)S(1)}, f32[768]{0:T(1024)}, u32[]{:S(2)}) copy-start(f32[768]{0:T(1024)} %param.40) | copy-start | bytes 9220
  373.5 103.1 %copy-start.47 = (f32[768]{0:T(1024)S(1)}, f32[768]{0:T(1024)}, u32[]{:S(2)}) copy-start(f32[768]{0:T(1024)} %param.39) | copy-start | bytes 9220
  373.5 103.1 %copy-start.49 = (f32[512]{0:T(512)S(1)}, f32[512]{0:T(512)}, u32[]{:S(2)}) copy-start(f32[512]{0:T(512)} %copy-done.48) | copy-start | bytes 6148
  476.6 3.5 copy-start.39
  476.6 4.4 copy-start.40
  (18 other events, 29.3 us)

commit v2 on v1

--- a/solution.py
+++ b/solution.py
@@ -1,4 +1,3 @@
-import functools
 import math
 
 import jax
@@ -661,48 +660,357 @@
     )(part_f, part_q, out_low, grad_low, vec)
 
 
-def pair_kernel(own, both, send_sem, recv_sem, local):
+ROWS = 512
+SCALE = 0.125
+BQ, BV, BO, BD, G1, S1, G2, S2, ZH, BU, ZI, SC = 0, 1, 2, 3, 4, 5, 6, 7, 8, 9, 13, 17
+ROOT_HALF = math.sqrt(0.5)
+DENSITY = 1.0 / math.sqrt(2.0 * math.pi)
+
+
+def smem_spec():
+    return pl.BlockSpec(memory_space=pltpu.SMEM)
+
+
+def vmem(shape, dtype):
+    return pltpu.VMEM(shape, dtype)
+
+
+def stack_head(rows, half):
+    blank = jnp.zeros_like(rows)
+    return jnp.concatenate([rows, blank] if half == 0 else [blank, rows], axis=0)
+
+
+def key_mask(mask, length):
+    row = lax.broadcasted_iota(jnp.int32, mask.shape, 0)
+    mask[...] = jnp.where(row < length, 0.0, -1e30)
+
+
+def attend_kernel(
+    length, z_head, x, w, bq, bv, q, qt, k, kt, v, ot, ctx, lse, vt, mask, send, recv
+):
     d = Around()
+    c = d.c
     greet([d.sibling])
-    copy = remote(own, both.at[d.c], send_sem.at[0], recv_sem.at[0], d.sibling)
-    copy.start()
-    keep = pltpu.make_async_copy(own, both.at[d.c], local.at[0])
-    keep.start()
-    keep.wait()
-    copy.wait_send()
-    remote(own, both.at[1 - d.c], send_sem.at[0], recv_sem.at[0], d.sibling).wait_recv()
-
-
-def pair(own):
+    xv = x[...]
+
+    def share(i, buf):
+        copy = remote(buf.at[c], buf.at[c], send.at[i], recv.at[i], d.sibling)
+        copy.start()
+        return copy
+
+    keys = times_trans(xv, w[1])
+    k[c] = keys.astype(BF16)
+    copies = [share(0, k)]
+    kt[c] = keys.T.astype(BF16)
+    copies.append(share(1, kt))
+    values = times_trans(xv, w[2]) + bv[...]
+    v[c] = values.astype(BF16)
+    copies.append(share(2, v))
+    vt[c] = values.T.astype(BF16)
+    copies.append(share(3, vt))
+    query = (times_trans(xv, w[0]) + bq[...]) * SCALE
+    q[...] = query.astype(BF16)
+    qt[...] = query.T.astype(BF16)
+    key_mask(mask, length[0])
+    for i, buf in enumerate((k, kt, v, vt)):
+        remote(buf.at[1 - c], buf.at[1 - c], send.at[i], recv.at[i], d.sibling).wait_recv()
+    for copy in copies:
+        copy.wait_send()
+
+    def pair_body(p, carry):
+        lanes = pl.ds(pl.multiple_of(p * 128, 128), 128)
+        kp = k[:, :, lanes].reshape(2 * ROWS, 128)
+        off = jnp.concatenate([mask[...]] * 4, axis=1)
+        for half in (0, 1):
+            h = p * 2 + half
+            span = pl.ds(pl.multiple_of(h * 64, 64), 64)
+            s = times_plain(kp, stack_head(qt[span, :], half)) + off
+            top = jnp.max(s, axis=0, keepdims=True)
+            e = jnp.exp(s - top)
+            den = jnp.sum(e, axis=0, keepdims=True)
+            probs = (e * (1.0 / den)).astype(BF16)
+            ot[span, :] = times_plain(vt[0, span, :], probs[:ROWS]) + times_plain(
+                vt[1, span, :], probs[ROWS:]
+            )
+            lse[pl.ds(h, 1), :] = top + jnp.log(den)
+        return carry
+
+    lax.fori_loop(0, HEADS // 2, pair_body, 0)
+    for h in range(HEADS):
+        span = slice(h * 64, h * 64 + 64)
+        ctx[:, span] = (ot[span, :] * z_head[h]).T.astype(BF16)
+
+
+def attend(length, z_head, x, w, bq, bv):
     return pl.pallas_call(
-        pair_kernel,
-        out_shape=shaped((2,) + own.shape, own.dtype),
-        in_specs=[any_spec()],
-        out_specs=any_spec(),
-        scratch_shapes=[dma(1), dma(1), dma(1)],
-        compiler_params=pltpu.CompilerParams(collective_id=3, has_side_effects=True),
-        name="pair",
-    )(own)
-
-
-def trade_kernel(parts, other, send_sem, recv_sem):
+        attend_kernel,
+        out_shape=(
+            shaped((ROWS, D), BF16),
+            shaped((D, ROWS), BF16),
+            shaped((2, ROWS, D), BF16),
+            shaped((2, D, ROWS), BF16),
+            shaped((2, ROWS, D), BF16),
+            shaped((D, ROWS), F32),
+            shaped((ROWS, D), BF16),
+            shaped((HEADS, ROWS), F32),
+        ),
+        in_specs=[smem_spec()] * 2 + [vmem_spec()] * 4,
+        out_specs=(vmem_spec(),) * 8,
+        scratch_shapes=[vmem((2, D, ROWS), BF16), vmem((2 * ROWS, 128), F32), dma(4), dma(4)],
+        compiler_params=pltpu.CompilerParams(
+            collective_id=5, has_side_effects=True, vmem_limit_bytes=60 << 20
+        ),
+        name="attend",
+    )(length, z_head, x, w, bq, bv)
+
+
+def rows_loop(body, step=128):
+    def run(i, carry):
+        body(i * step, pl.ds(pl.multiple_of(i * step, step), step))
+        return carry
+
+    lax.fori_loop(0, ROWS // step, run, 0)
+
+
+def col_sum(values):
+    return jnp.sum(values, axis=0, keepdims=True)
+
+
+def row_mean(values):
+    return jnp.sum(values, axis=1, keepdims=True) * (1.0 / D)
+
+
+def mid_kernel(
+    length, count, zm, zf, z_head,
+    x, t, ctx, ot, wo, wu, wd, bo, bu, bd, g1, s1, g2, s2, zh, zi,
+    out, dwu, dwd, dwo, gfirst, g, gt, vec,
+    attn, fn, xh1, r1, low, up, cdf, hid, gsec, gdown, acc,
+):
+    c = lax.axis_index("dp") % 2
+    vec[...] = jnp.zeros_like(vec)
+    lane = lax.broadcasted_iota(jnp.int32, (1, D), 1)
+
+    def add(row, value):
+        vec[row : row + 1, :] += value
+
+    def add_scalar(at, value):
+        vec[SC : SC + 1, :] += jnp.where(lane == at, value, 0.0)
+
+    attn[...] = times_plain(ctx[...], wo[...]) + bo[...]
+    ba = zm[0] * zh[...]
+    bf = zf[0] * zh[...]
+
+    def first(at, span):
+        h = x[span, :].astype(F32) + ba * attn[span, :]
+        cen = h - row_mean(h)
+        r = lax.rsqrt(row_mean(cen * cen) + epsilon)
+        xh = cen * r
+        xh1[span, :] = xh
+        r1[span, :] = jnp.broadcast_to(r, (128, 128))
+        f = xh * g1[...] + s1[...]
+        fn[span, :] = f
+        low[span, :] = f.astype(BF16)
+
+    rows_loop(first)
+    acc[...] = jnp.zeros_like(acc)
+
+    def unit_fwd(j, carry):
+        units = pl.ds(pl.multiple_of(j * D, D), D)
+        u = times_trans(low[...], wu[units, :]) + bu[:, units]
+        up[:, units] = u
+        cd = 0.5 * (1.0 + lax.erf(u * ROOT_HALF))
+        cdf[:, units] = cd
+        hv = (u * cd * zi[:, units]).astype(BF16)
+        hid[:, units] = hv
+        acc[...] += times_plain(hv, wd[units, :])
+        return carry
+
+    lax.fori_loop(0, FF // D, unit_fwd, 0)
+    scale = (2.0 * 32 * ROWS) / count[0]
+
+    def second(at, span):
+        down = acc[span, :] + bd[...]
+        h = fn[span, :] + bf * down
+        cen = h - row_mean(h)
+        r = lax.rsqrt(row_mean(cen * cen) + epsilon)
+        xh = cen * r
+        o = xh * g2[...] + s2[...]
+        out[span, :] = o
+        pos = lax.broadcasted_iota(jnp.int32, (128, D), 0) + (c * ROWS + at)
+        res = jnp.where(pos < length[0], o - t[span, :].astype(F32), 0.0)
+        add_scalar(14, jnp.sum(res * res))
+        go = res * scale
+        add(G2, col_sum(go * xh))
+        add(S2, col_sum(go))
+        e = go * g2[...]
+        gs = r * (e - row_mean(e) - xh * row_mean(e * xh))
+        gsec[span, :] = gs
+        gd = (gs * bf).astype(BF16)
+        gdown[span, :] = gd
+        add(BD, col_sum(gd.astype(F32)))
+        gsd = gs * down
+        add_scalar(13, jnp.sum(gsd * zh[...]))
+        add(ZH, col_sum(gsd * zf[0]))
+
+    rows_loop(second)
+    acc[...] = gsec[...]
+
+    def unit_bwd(j, carry):
+        units = pl.ds(pl.multiple_of(j * D, D), D)
+        gh = times_trans(gdown[...], wd[units, :])
+        u = up[:, units]
+        cd = cdf[:, units]
+        vec[pl.ds(ZI + j, 1), :] = col_sum(gh * (u * cd))
+        gu = (gh * zi[:, units] * (cd + u * (DENSITY * jnp.exp(-0.5 * u * u)))).astype(BF16)
+        vec[pl.ds(BU + j, 1), :] = col_sum(gu.astype(F32))
+        acc[...] += times_plain(gu, wu[units, :])
+        dwd[units, :] = trans_times(hid[:, units], gdown[...]).astype(BF16)
+        dwu[units, :] = trans_times(gu, low[...]).astype(BF16)
+        return carry
+
+    lax.fori_loop(0, FF // D, unit_bwd, 0)
+
+    def third(at, span):
+        gf = acc[span, :]
+        xh = xh1[span, :]
+        add(G1, col_sum(gf * xh))
+        add(S1, col_sum(gf))
+        e = gf * g1[...]
+        gr = r1[span, 0:1] * (e - row_mean(e) - xh * row_mean(e * xh))
+        gfirst[span, :] = gr
+        ga = (gr * ba).astype(BF16)
+        low[span, :] = ga
+        add(BO, col_sum(ga.astype(F32)))
+        gra = gr * attn[span, :]
+        add_scalar(12, jnp.sum(gra * zh[...]))
+        add(ZH, col_sum(gra * zm[0]))
+
+    rows_loop(third)
+    dwo[...] = trans_times(ctx[...], low[...]).astype(BF16)
+    gct = times_trans(wo[...], low[...])
+    for h in range(HEADS):
+        span = slice(h * 64, h * 64 + 64)
+        block = gct[span, :]
+        add_scalar(h, jnp.sum(block * ot[span, :]))
+        gb = block * z_head[h]
+        gt[span, :] = gb.astype(BF16)
+        g[:, span] = gb.T.astype(BF16)
+
+
+def mid(length, count, zm, zf, z_head, *arrays):
+    return pl.pallas_call(
+        mid_kernel,
+        out_shape=(
+            shaped((ROWS, D), F32),
+            shaped((FF, D), BF16),
+            shaped((FF, D), BF16),
+            shaped((D, D), BF16),
+            shaped((ROWS, D), F32),
+            shaped((ROWS, D), BF16),
+            shaped((D, ROWS), BF16),
+            shaped((24, D), F32),
+        ),
+        in_specs=[smem_spec()] * 5 + [vmem_spec()] * len(arrays),
+        out_specs=(vmem_spec(),) * 8,
+        scratch_shapes=[
+            vmem((ROWS, D), F32),
+            vmem((ROWS, D), F32),
+            vmem((ROWS, D), F32),
+            vmem((ROWS, 128), F32),
+            vmem((ROWS, D), BF16),
+            vmem((ROWS, FF), F32),
+            vmem((ROWS, FF), F32),
+            vmem((ROWS, FF), BF16),
+            vmem((ROWS, D), F32),
+            vmem((ROWS, D), BF16),
+            vmem((ROWS, D), F32),
+        ],
+        compiler_params=pltpu.CompilerParams(vmem_limit_bytes=63 << 20),
+        name="mid",
+    )(length, count, zm, zf, z_head, *arrays)
+
+
+def back_kernel(
+    length, x, w, q, qt, k, kt, v, g, gt, ot, lse, gfirst, vec_in,
+    dw, gin, vec, dqt, dkp, dvp, mask, rk, rv, send, recv,
+):
     d = Around()
+    c = d.c
     greet([d.sibling])
-    copy = remote(parts.at[1 - d.c], other, send_sem.at[0], recv_sem.at[0], d.sibling)
-    copy.start()
-    copy.wait()
-
-
-def trade(parts):
+    key_mask(mask, length[0])
+    lane = lax.broadcasted_iota(jnp.int32, (ROWS, 128), 1)
+
+    def pair_body(p, carry):
+        lanes = pl.ds(pl.multiple_of(p * 128, 128), 128)
+        kp = k[:, :, lanes].reshape(2 * ROWS, 128)
+        vp = v[:, :, lanes].reshape(2 * ROWS, 128)
+        qp = q[:, lanes]
+        gp = g[:, lanes]
+        off = jnp.concatenate([mask[...]] * 4, axis=1)
+        zero = jnp.zeros_like(qp)
+        dka = []
+        dva = []
+        for half in (0, 1):
+            h = p * 2 + half
+            span = pl.ds(pl.multiple_of(h * 64, 64), 64)
+            mine = (lane >= 64) if half else (lane < 64)
+            s = times_plain(kp, stack_head(qt[span, :], half)) + off
+            probs = jnp.exp(s - lse[pl.ds(h, 1), :])
+            gth = gt[span, :]
+            gp_t = times_plain(vp, stack_head(gth, half))
+            dots = col_sum(gth.astype(F32) * ot[span, :])
+            ds = (probs * (gp_t - dots)).astype(BF16)
+            dka.append(times_plain(ds, jnp.where(mine, qp, zero)))
+            dva.append(times_plain(probs.astype(BF16), jnp.where(mine, gp, zero)))
+            dq = times_plain(kt[0, span, :], ds[:ROWS]) + times_plain(kt[1, span, :], ds[ROWS:])
+            dqt[span, :] = (dq * SCALE).astype(BF16)
+        dkp[:, :, lanes] = (dka[0] + dka[1]).reshape(2, ROWS, 128)
+        dvp[:, :, lanes] = (dva[0] + dva[1]).reshape(2, ROWS, 128)
+        return carry
+
+    lax.fori_loop(0, HEADS // 2, pair_body, 0)
+    copies = [
+        remote(dkp.at[1 - c], rk, send.at[0], recv.at[0], d.sibling),
+        remote(dvp.at[1 - c], rv, send.at[1], recv.at[1], d.sibling),
+    ]
+    for copy in copies:
+        copy.start()
+    dw[0] = times_plain(dqt[...], x[...]).astype(BF16)
+    dq = dqt[...].astype(F32).T
+    vec[...] = vec_in[...]
+    vec[BQ : BQ + 1, :] = col_sum(dq)
+    total = gfirst[...] + times_plain(dq.astype(BF16), w[0])
+    for copy in copies:
+        copy.wait()
+    dk = (dkp[c] + rk[...]).astype(BF16)
+    dv = (dvp[c] + rv[...]).astype(BF16)
+    vec[BV : BV + 1, :] = col_sum(dv.astype(F32))
+    dw[1] = trans_times(dk, x[...]).astype(BF16)
+    dw[2] = trans_times(dv, x[...]).astype(BF16)
+    gin[...] = total + times_plain(dk, w[1]) + times_plain(dv, w[2])
+
+
+def back(length, *arrays):
     return pl.pallas_call(
-        trade_kernel,
-        out_shape=shaped(parts.shape[1:], parts.dtype),
-        in_specs=[any_spec()],
-        out_specs=any_spec(),
-        scratch_shapes=[dma(1), dma(1)],
-        compiler_params=pltpu.CompilerParams(collective_id=4, has_side_effects=True),
-        name="trade",
-    )(parts)
+        back_kernel,
+        out_shape=(shaped((3, D, D), BF16), shaped((ROWS, D), F32), shaped((24, D), F32)),
+        in_specs=[smem_spec()] + [vmem_spec()] * len(arrays),
+        out_specs=(vmem_spec(),) * 3,
+        scratch_shapes=[
+            vmem((D, ROWS), BF16),
+            vmem((2, ROWS, D), F32),
+            vmem((2, ROWS, D), F32),
+            vmem((2 * ROWS, 128), F32),
+            vmem((ROWS, D), F32),
+            vmem((ROWS, D), F32),
+            dma(2),
+            dma(2),
+        ],
+        compiler_params=pltpu.CompilerParams(
+            collective_id=6, has_side_effects=True, vmem_limit_bytes=63 << 20
+        ),
+        name="back",
+    )(length, *arrays)
 
 
 def by_chip(
@@ -731,168 +1039,44 @@
     z_ffn,
 ):
     z, x, core, y = place()
-    rows = inputs.shape[0]
-    head_size = D // HEADS
-    softmax_scale = 1.0 / math.sqrt(head_size)
     halves = jnp.concatenate([lengths // 32, lengths % 32]).astype(BF16)
     marks = jnp.pad(halves[None, :], ((0, 7), (0, D - 2)))
     pack1 = jnp.concatenate([w_query, w_key, w_value, marks], axis=0)
     pack2 = jnp.concatenate([w_up, w_down, w_out], axis=0)
     source, target, full1, full2 = gather_all(inputs, teacher, pack1, pack2)
-    wq = full1[:, 0:24].reshape(D, D)
-    wk = full1[:, 24:48].reshape(D, D)
-    wv = full1[:, 48:72].reshape(D, D)
+    wqkv = jnp.stack([full1[:, i * 24 : i * 24 + 24].reshape(D, D) for i in range(3)])
     wu = full2[:, 0:96].reshape(FF, D)
     wd = full2[:, 96:192].reshape(FF, D)
     wo = full2[:, 192:216].reshape(D, D)
     marks_all = full1[:16, 72, 0:2].astype(F32)
     lengths_all = marks_all[:, 0] * 32.0 + marks_all[:, 1]
-    valid_count = jnp.sum(lengths_all)
-    length = lengths_all[z * 4 + x * 2 + y]
-    valid_keys = jnp.arange(SEQ, dtype=jnp.int32).astype(F32) < length
-    positions = core * rows + jnp.arange(rows, dtype=jnp.int32)
-    valid_own = positions.astype(F32) < length
-
-    query = ((times_trans(source, wq) + b_query) * softmax_scale).astype(BF16)
-    keys_own = times_trans(source, wk).astype(BF16)
-    values_own = (times_trans(source, wv) + b_value).astype(BF16)
-    kv = pair(jnp.concatenate([keys_own, values_own], axis=1)).reshape(SEQ, 2 * D)
-    query3 = query.reshape(rows, HEADS, head_size)
-    keys3 = kv[:, :D].reshape(SEQ, HEADS, head_size)
-    values3 = kv[:, D:].reshape(SEQ, HEADS, head_size)
-    scores = jnp.einsum("qhd,khd->hqk", query3, keys3, preferred_element_type=F32)
-    scores = jnp.where(valid_keys[None, None, :], scores, -1e30)
-    highest = jnp.max(scores, axis=-1, keepdims=True)
-    exponent = jnp.exp(scores - highest)
-    denominator = jnp.sum(exponent, axis=-1, keepdims=True)
-    attention = exponent / denominator
-    attention_b = attention.astype(BF16)
-    context_f = jnp.einsum("hqk,khd->qhd", attention_b, values3, preferred_element_type=F32)
-    gated = (context_f * z_head[None, :, None]).reshape(rows, D).astype(BF16)
-
-    attn_out = times_plain(gated, wo) + b_out
-    branch_attn = z_mha * z_hidden
-    first_sum = source.astype(F32) + branch_attn * attn_out
-    first_norm = norm_rows(first_sum, gain_one, shift_one)
-    first_low = first_norm.astype(BF16)
-    upper = times_trans(first_low, wu) + b_up
-    activated = gelu_exact(upper)
-    hidden_b = (activated * z_int).astype(BF16)
-    down = times_plain(hidden_b, wd) + b_down
-    branch_ffn = z_ffn * z_hidden
-    second_sum = first_norm + branch_ffn * down
-    output = norm_rows(second_sum, gain_two, shift_two)
-    residue = output - target.astype(F32)
-    masked = jnp.where(valid_own[:, None], residue, 0.0)
-    square_sum = jnp.sum(masked * masked)
-    tokens_all = rows * 32
-    grad_out = masked * (2.0 * tokens_all / valid_count)
-    unused, pull_two = jax.vjp(norm_rows, second_sum, gain_two, shift_two)
-    grad_second, grad_gain_two, grad_shift_two = pull_two(grad_out)
-    grad_down = (grad_second * branch_ffn).astype(BF16)
-    grad_z_ffn = jnp.sum(grad_second * z_hidden * down).reshape(1)
-    hidden_part = jnp.sum(grad_second * z_ffn * down, axis=0)
-    grad_b_down = jnp.sum(grad_down.astype(F32), axis=0)
-    grad_w_down = trans_times(hidden_b, grad_down).astype(BF16)
-    grad_hidden = times_trans(grad_down, wd)
-    grad_z_int = jnp.sum(grad_hidden * activated, axis=0)
-    unused, gelu_pull = jax.vjp(gelu_exact, upper)
-    grad_upper = gelu_pull(grad_hidden * z_int)[0].astype(BF16)
-    grad_b_up = jnp.sum(grad_upper.astype(F32), axis=0)
-    grad_w_up = trans_times(grad_upper, first_low).astype(BF16)
-    grad_first_norm = grad_second + times_plain(grad_upper, wu)
-    unused, pull_one = jax.vjp(norm_rows, first_sum, gain_one, shift_one)
-    grad_first, grad_gain_one, grad_shift_one = pull_one(grad_first_norm)
-    grad_attn = (grad_first * branch_attn).astype(BF16)
-    grad_z_mha = jnp.sum(grad_first * z_hidden * attn_out).reshape(1)
-    hidden_part = hidden_part + jnp.sum(grad_first * z_mha * attn_out, axis=0)
-    grad_b_out = jnp.sum(grad_attn.astype(F32), axis=0)
-    grad_w_out = trans_times(gated, grad_attn).astype(BF16)
-    grad_gated = times_trans(grad_attn, wo).reshape(rows, HEADS, head_size)
-    grad_z_head = jnp.sum(grad_gated * context_f, axis=(0, 2))
-    grad_heads = (grad_gated * z_head[None, :, None]).astype(BF16)
-
-    grad_attention = jnp.einsum(
-        "qhd,khd->hqk", grad_heads, values3, preferred_element_type=F32
-    )
-    row_dots = jnp.sum(attention * grad_attention, axis=-1, keepdims=True)
-    grad_scores = (attention * (grad_attention - row_dots)).astype(BF16)
-    grad_query = (
-        softmax_scale
-        * jnp.einsum("hqk,khd->qhd", grad_scores, keys3, preferred_element_type=F32)
-    ).astype(BF16).reshape(rows, D)
-    grad_keys_part = jnp.einsum(
-        "hqk,qhd->khd", grad_scores, query3, preferred_element_type=F32
-    ).reshape(2, rows, D)
-    grad_values_part = jnp.einsum(
-        "hqk,qhd->khd", attention_b, grad_heads, preferred_element_type=F32
-    ).reshape(2, rows, D)
-    parts = jnp.concatenate([grad_keys_part, grad_values_part], axis=2)
-    own_parts = lax.dynamic_index_in_dim(parts, core, 0, keepdims=False)
-    grad_kv = (own_parts + trade(parts)).astype(BF16)
-    grad_keys, grad_values = grad_kv[:, :D], grad_kv[:, D:]
-    grad_w_query = trans_times(grad_query, source).astype(BF16)
-    grad_w_key = trans_times(grad_keys, source).astype(BF16)
-    grad_w_value = trans_times(grad_values, source).astype(BF16)
-    grad_b_query = jnp.sum(grad_query.astype(F32), axis=0)
-    grad_b_value = jnp.sum(grad_values.astype(F32), axis=0)
-    grad_inputs = (
-        grad_first
-        + times_plain(grad_query, wq)
-        + times_plain(grad_keys, wk)
-        + times_plain(grad_values, wv)
+    valid_count = jnp.sum(lengths_all).reshape(1)
+    length = lengths_all[z * 4 + x * 2 + y].astype(jnp.int32).reshape(1)
+    row = lambda a: a.reshape(1, -1)
+    q, qt, k, kt, v, ot, ctx, lse = attend(
+        length, z_head, source, wqkv, row(b_query), row(b_value)
+    )
+    output, dwu, dwd, dwo, gfirst, g, gt, vec = mid(
+        length, valid_count, z_mha, z_ffn, z_head,
+        source, target, ctx, ot, wo, wu, wd, row(b_out), row(b_up), row(b_down),
+        row(gain_one), row(shift_one), row(gain_two), row(shift_two), row(z_hidden), row(z_int),
+    )
+    dw, grad_inputs, vec = back(
+        length, source, wqkv, q, qt, k, kt, v, g, gt, ot, lse, gfirst, vec
     )
     part_f = jnp.concatenate(
-        [
-            grad_w_up.reshape(32, 96, D),
-            grad_w_down.reshape(32, 96, D),
-            grad_w_out.reshape(32, 24, D),
-        ],
-        axis=1,
-    )
-    part_q = jnp.concatenate(
-        [
-            grad_w_query.reshape(32, 24, D),
-            grad_w_key.reshape(32, 24, D),
-            grad_w_value.reshape(32, 24, D),
-        ],
-        axis=1,
-    )
-    pieces = (
-        grad_b_query,
-        grad_b_value,
-        grad_b_out,
-        grad_b_down,
-        grad_gain_one,
-        grad_shift_one,
-        grad_gain_two,
-        grad_shift_two,
-        hidden_part,
-        grad_b_up,
-        grad_z_int,
-        grad_z_head,
-        grad_z_mha,
-        grad_z_ffn,
-        square_sum.reshape(1),
-    )
-    flat = jnp.concatenate(pieces)
-    vec = jnp.pad(flat, (0, 104 * 128 - flat.shape[0])).reshape(104, 128)
-    sum_f, sum_q, out_swap, grad_swap, vec_sum = scatter_all(
+        [dwu.reshape(32, 96, D), dwd.reshape(32, 96, D), dwo.reshape(32, 24, D)], axis=1
+    )
+    part_q = jnp.concatenate([dw[i].reshape(32, 24, D) for i in range(3)], axis=1)
+    sum_f, sum_q, out_swap, grad_swap, sums = scatter_all(
         part_f, part_q, output.astype(BF16), grad_inputs.astype(BF16), vec
     )
-    total = vec_sum.reshape(-1)
-    sums = []
-    at = 0
-    for piece in pieces:
-        sums.append(total[at : at + piece.shape[0]])
-        at += piece.shape[0]
     home = core == y
     layer_out = jnp.where(home, output, out_swap.astype(F32))
     grad_home = jnp.where(home, grad_inputs, grad_swap.astype(F32))
-    (s_bq, s_bv, s_bo, s_bd, s_g1, s_s1, s_g2, s_s2, s_zh, s_bu, s_zi, s_hd, s_zm, s_zf, s_sq) = sums
     return (
         layer_out,
-        s_sq / (D * valid_count),
+        sums[SC, 14:15] / (D * valid_count),
         grad_home,
         sum_q[0:24],
         sum_q[24:48],
@@ -900,20 +1084,20 @@
         sum_f[192:216],
         sum_f[0:96],
         sum_f[96:192],
-        s_bq,
-        s_bv,
-        s_bo,
-        s_bu,
-        s_bd,
-        s_g1,
-        s_s1,
-        s_g2,
-        s_s2,
-        s_hd,
-        s_zm,
-        s_zh,
-        s_zi,
-        s_zf,
+        sums[BQ],
+        sums[BV],
+        sums[BO],
+        sums[BU : BU + 4].reshape(-1),
+        sums[BD],
+        sums[G1],
+        sums[S1],
+        sums[G2],
+        sums[S2],
+        sums[SC, 0:12],
+        sums[SC, 12:13],
+        sums[ZH],
+        sums[ZI : ZI + 4].reshape(-1),
+        sums[SC, 13:14],
     )
 
 

time: 492 us -> 350 us (0.71)
  matrix products: 127 us -> 0 us
  Pallas kernels: 246 us -> 288 us
  other arithmetic: 50.9 us -> 24.4 us
  local copies, waits for them, and re-layouts: 54.3 us -> 29.6 us
    dot_general x23 -> x0, matrix products: 115 us -> none  [the longest x6 33.8 us: times_trans(): lax.dot_general(left, right, (((1,), (1,)), ((), ())), preferred_element_...]
    pallas_call x2 -> x3, Pallas kernels: 55.3 us -> 96.8 us  [the longest x1 39.1 us: mid(): pl.pallas_call(mid_kernel, out_shape=(shaped((ROWS, D), F32), shaped((FF,...]
    convert_element_type x2 -> x3, other arithmetic: 19 us -> 2.5 us  [the longest x1 0.96 us: by_chip(): grad_inputs.astype(BF16)]
    sub x1 -> x0, matrix products: 12.8 us -> none  [by_chip(): exponent = jnp.exp(scores - highest)]
    reduce_sum x9 -> x1, other arithmetic: 9.19 us -> 0.6 us  [by_chip(): valid_count = jnp.sum(lengths_all).reshape(1)]
    unnamed x132 -> x12, local copies, waits for them, and re-layouts: 8.15 us -> 0.18 us
    slice x8 -> x5, local copies, waits for them, and re-layouts: 11.4 us -> 3.71 us  [the longest x1 2.22 us: by_chip(): full1[:, i * 24:i * 24 + 24].reshape(D, D)]
    reshape x5 -> x11, local copies, waits for them, and re-layouts: 20.2 us -> 12.6 us  [the longest x9 11.4 us: by_chip(): row = lambda a: a.reshape(1, -1)]
where the time goes in v2:
time: 350 us; the launch traced here: 348 us
  Pallas kernels  288 us (82%)
  local copies, waits for them, and re-layouts  29.6 us (8%)
  other arithmetic  24.4 us (7%)
  between operations  5.24 us (1%)
    pallas_call x1, Pallas kernels, scatter_all(): pl.pallas_call(scatter_kernel, out_shape=(shaped((216, D), F32), shaped((...  101 us
    pallas_call x1, Pallas kernels, gather_all(): pl.pallas_call(gather_kernel, out_shape=(shaped(inputs.shape, BF16), shap...  90.3 us
    pallas_call x1, Pallas kernels, mid(): pl.pallas_call(mid_kernel, out_shape=(shaped((ROWS, D), F32), shaped((FF,...  39.1 us
    pallas_call x1, Pallas kernels, back(): pl.pallas_call(back_kernel, out_shape=(shaped((3, D, D), BF16), shaped((R...  33.2 us
    pallas_call x1, Pallas kernels, attend(): pl.pallas_call(attend_kernel, out_shape=(shaped((ROWS, D), BF16), shaped(...  24.5 us
    reshape x9, local copies, waits for them, and re-layouts, by_chip(): row = lambda a: a.reshape(1, -1)  11.4 us
    concatenate x1, other arithmetic, by_chip(): jnp.concatenate([dwu.reshape(32, 96, D), dwd.reshape(32, 96, D), dwo.resh...  9.74 us
    slice x1, local copies, waits for them, and re-layouts, by_chip(): wd = full2[:, 96:192].reshape(FF, D)  7.96 us

profile of v2, /device:TPU:6, one launch (start us, length us, event | category | flops | bytes accessed | tf_op | source)
XLA Modules:
  0.0 347.6 jit_solution(6634055874729534260)
XLA Ops:
  2.7 1.3 reshape.152.bq
  4.0 1.3 reshape.153.bv
  5.2 1.3 reshape.157.bo
  6.5 1.3 reshape.159.bd
  7.8 1.3 reshape.160.g1
  9.0 1.3 reshape.161.s1
  10.3 1.3 reshape.162.g2
  11.6 1.3 reshape.163.s2
  12.8 1.3 reshape.164.zh
  14.1 0.1 fusion.5
  14.2 1.5 pad_maximum_fusion.4.p1
  15.6 1.8 pad_maximum_fusion.3.p2
  17.4 90.3 %gather_all.1 = (bf16[512,768]{1,0:T(8,128)(2,1)}, bf16[512,768]{1,0:T(8,128)(2,1)}, bf16[32,80,768]{2,1,0:T(8,128)(2,1)}, bf16[32,216,768]{2,1,0:T(8,128)(2,1)}) custom-call(bf16[512,768]{1,0:T(8,128)(2,1)} %x_in.1, bf16[512,768]{1,0:T(8,128)(2,1)} %t_in.1, bf16[80,768]{1,0:T(8,128)(2,1)} %pad_maximum_fusion.4.p1, bf16[216,768]{1,0:T(8,128)(2,1)} %pad_maximum_fusion.3.p2), custom_call_target="tpu_custom_call" | custom-call | tf_op jit(solution)/shard_map/gather_all/pallas_call | solution.py:490
  107.7 0.8 slice_convert_fusion
  108.4 2.2 fusion.8
  110.7 0.1 copy.47
  110.7 2.0 pad_maximum_fusion.1.w
  112.7 0.6 fusion.6
  114.0 0.6 fusion.14
  114.6 2.4 slice.105
  116.9 8.0 %fusion.7 = (bf16[32,96,768]{2,1,0:T(8,128)(2,1)}, bf16[32,96,768]{2,1,0:T(8,128)(2,1)}) fusion(bf16[32,216,768]{2,1,0:T(8,128)(2,1)} %get-tuple-element.56), kind=kLoop, calls=%fused_computation.29 | loop fusion | bytes 18874368 | tf_op jit(solution)/shard_map/slice | solution.py:1049
  124.9 24.5 %attend.1 = (bf16[512,768]{1,0:T(8,128)(2,1)}, bf16[768,512]{1,0:T(8,128)(2,1)}, bf16[2,512,768]{2,1,0:T(8,128)(2,1)}, bf16[2,768,512]{2,1,0:T(8,128)(2,1)}, bf1...) custom-call(s32[1]{0:T(128)} %bitcast.3.length, f32[12]{0:T(128)} %z_head.3, ...), custom_call_target="tpu_custom_call" | custom-call | tf_op jit(solution)/shard_map/attend/pallas_call | solution.py:745
  149.5 39.1 %mid.1 = (f32[512,768]{1,0:T(8,128)}, bf16[3072,768]{1,0:T(8,128)(2,1)}, bf16[3072,768]{1,0:T(8,128)(2,1)}, bf16[768,768]{1,0:T(8,128)(2,1)}, f32[512,768]{1,0:T...) custom-call(s32[1]{0:T(128)} %bitcast.3.length, f32[1]{0:T(128)} %bitcast.4.count, ...), custom_call_target="tpu_custom_call" | custom-call | tf_op jit(solution)/shard_map/mid/pallas_call | solution.py:901
  188.6 33.2 %back.1 = (bf16[3,768,768]{2,1,0:T(8,128)(2,1)}, f32[512,768]{1,0:T(8,128)}, f32[24,768]{1,0:T(8,128)}) custom-call(s32[1]{0:T(128)} %bitcast.3.length, bf16[512,768]{1,0:T(8,128)(2,1)} %get-tuple-element.52.x, bf16[3,768,768]{2,1,0:T(8,128)(2,1)} %pad_maximum_fusion.1.w, bf16[512,768]{1,0:T(8,128)(2,1)} %get-tuple-element.61.q, ...), custom_call_target="tpu_custom_call" | custom-call | tf_op jit(solution)/shard_map/back/pallas_call | solution.py:994
  221.8 0.0 copy-start.2
  221.8 9.7 %pad_maximum_fusion.part_f = bf16[32,216,768]{2,1,0:T(8,128)(2,1)} fusion(bf16[32,24,768]{2,1,0:T(8,128)(2,1)} %bitcast.35, bf16[32,96,768]{2,1,0:T(8,128)(2,1)} %bitcast.34, bf16[32,96,768]{2,1,0:T(8,128)(2,1)} %bitcast.33), kind=kLoop, calls=%fused_computation | loop fusion | flops 31850496 | bytes 21233664 | tf_op jit(solution)/shard_map/concatenate | solution.py:1067
  231.5 0.0 copy-done.2
  231.5 0.2 fusion.9
  231.7 0.0 copy-start.1
  231.8 0.0 copy-start
  231.8 2.0 pad_maximum_fusion.2.part_q
  233.8 0.1 copy-done.1
  233.9 1.0 convert_element_type.40.grad_in
  234.8 0.1 copy-done
  234.9 1.0 convert_element_type.39.out_in
  235.9 101.2 %scatter_all.1 = (f32[216,768]{1,0:T(8,128)}, f32[72,768]{1,0:T(8,128)}, bf16[512,768]{1,0:T(8,128)(2,1)}, bf16[512,768]{1,0:T(8,128)(2,1)}, f32[24,768]{1,0:T(8,128)}) custom-call(bf16[32,216,768]{2,1,0:T(8,128)(2,1)} %pad_maximum_fusion.part_f, bf16[32,72,768]{2,1,0:T(8,128)(2,1)} %pad_maximum_fusion.2.part_q, ...), custom_call_target="tpu_custom_call" | custom-call | tf_op jit(solution)/shard_map/scatter_all/pallas_call | solution.py:639
  337.1 0.0 copy-start.5
  337.1 0.0 copy-start.3
  337.1 0.0 copy-start.4
  337.1 3.4 convert_select_fusion
  340.6 0.5 slice_bitcast_fusion
  341.1 0.6 fusion.12
  342.4 0.7 slice_reduce_fusion
  343.0 0.6 reshape.170
  343.6 0.6 reshape.169
  344.3 0.6 slice.115
  344.9 0.8 fusion.10
  345.7 0.7 fusion.11
  (4 shorter events, 0.0 us)
Async XLA Ops:
  221.8 9.8 %copy-start.2 = (bf16[3,768,768]{2,1,0:T(8,128)(2,1)S(1)}, bf16[3,768,768]{2,1,0:T(8,128)(2,1)}, u32[]{:S(2)}) copy-start(bf16[3,768,768]{2,1,0:T(8,128)(2,1)} %get-tuple-element.71) | copy-start | bytes 10616836
  231.7 2.1 copy-start.1
  231.8 3.2 copy-start
  337.1 3.5 copy-start.5
  337.1 7.1 %copy-start.3 = (f32[216,768]{1,0:T(8,128)S(1)}, f32[216,768]{1,0:T(8,128)}, u32[]{:S(2)}) copy-start(f32[216,768]{1,0:T(8,128)} %get-tuple-element.78) | copy-start | bytes 1990660
  337.1 8.6 %copy-start.4 = (f32[72,768]{1,0:T(8,128)S(1)}, f32[72,768]{1,0:T(8,128)}, u32[]{:S(2)}) copy-start(f32[72,768]{1,0:T(8,128)} %get-tuple-element.77) | copy-start | bytes 663556

commit v3 on v0

--- a/solution.py
+++ b/solution.py
@@ -1,8 +1,11 @@
+import functools
 import math
 
 import jax
 import jax.numpy as jnp
 from jax import lax
+from jax.experimental import pallas as pl
+from jax.experimental.pallas import tpu as pltpu
 from jax.sharding import PartitionSpec as P
 
 D = 768
@@ -317,9 +320,909 @@
     )
 
 
+MESH = pl.DeviceIdType.MESH
+F32 = jnp.float32
+BF16 = jnp.bfloat16
+ROWS = 512
+SCALE = 0.125
+BQ, BV, BO, BD, G1, S1, G2, S2, ZH, BU, ZI, SC = 0, 1, 2, 3, 4, 5, 6, 7, 8, 9, 13, 17
+ROOT_HALF = math.sqrt(0.5)
+DENSITY = 1.0 / math.sqrt(2.0 * math.pi)
+
+
+def place():
+    dp = lax.axis_index("dp")
+    return dp // 4, (dp // 2) % 2, dp % 2, lax.axis_index("tensor")
+
+
+def device(z, x, c, y):
+    return ((z * 2 + x) * 2 + c, y)
+
+
+def shard_of(z, x, c, y):
+    return y * 16 + z * 4 + x * 2 + c
+
+
+def remote(src, dst, send_sem, recv_sem, to):
+    return pltpu.make_async_remote_copy(
+        src_ref=src,
+        dst_ref=dst,
+        send_sem=send_sem,
+        recv_sem=recv_sem,
+        device_id=to,
+        device_id_type=MESH,
+    )
+
+
+def greet(partners):
+    barrier = pltpu.get_barrier_semaphore()
+    for partner in partners:
+        pl.semaphore_signal(barrier, inc=1, device_id=partner, device_id_type=MESH)
+    pl.semaphore_wait(barrier, len(partners))
+
+
+def peers(axis):
+    return (1, 2, 3) if axis == "z" else (1,)
+
+
+def offsets(order):
+    found = [()]
+    for axis in order:
+        found = [o + (v,) for o in found for v in (0,) + peers(axis)]
+    return found
+
+
+class Around:
+    def __init__(self):
+        self.z, self.x, self.c, self.y = place()
+        self.sibling = device(self.z, self.x, 1 - self.c, self.y)
+        self.across = device(self.z, self.x, 1 - self.c, 1 - self.y)
+        self.all = [self.sibling, self.across]
+        self.all += [self.peer("z", v) for v in (1, 2, 3)] + [self.peer("x", 1), self.peer("y", 1)]
+
+    def at(self, order, offset, c):
+        z, x, y = self.z, self.x, self.y
+        for axis, v in zip(order, offset):
+            if v == 0:
+                continue
+            if axis == "z":
+                z = z ^ v
+            elif axis == "x":
+                x = 1 - x
+            elif axis == "y":
+                y = 1 - y
+            elif axis == "f":
+                x, y = x ^ c, y ^ (1 - c)
+            else:
+                x, y = x ^ (1 - c), y ^ c
+        return z, x, y
+
+    def peer(self, axis, v):
+        z, x, y = self.at(axis, (v,), self.c)
+        return device(z, x, self.c, y)
+
+    def shard(self, order, offset, c):
+        z, x, y = self.at(order, offset, c)
+        return shard_of(z, x, c, y)
+
+
+class Gather:
+    def __init__(self, d, order, own, full_at, send_sems, recv_sems):
+        self.d, self.order, self.own, self.full_at = d, order, own, full_at
+        self.send_sems, self.recv_sems = send_sems, recv_sems
+        self.slots = {o: i for i, o in enumerate(offsets(order))}
+        self.sent = 0
+        rest = [o for o in self.slots if any(o)]
+        rest.sort(key=lambda o: (sum(v > 0 for v in o), self.last(o), o))
+        self.events = [functools.partial(self.pass_on, o) for o in rest]
+
+    def last(self, offset):
+        return max(i for i, v in enumerate(offset) if v)
+
+    def send(self, src, shard, slot, to):
+        sem = self.send_sems.at[self.sent]
+        self.sent += 1
+        remote(src, self.full_at(shard), sem, self.recv_sems.at[slot], to).start()
+
+    def spread(self, src, offset, start):
+        shard = self.d.shard(self.order, offset, self.d.c)
+        for i in reversed(range(start, len(self.order))):
+            for v in peers(self.order[i]):
+                there = offset[:i] + (v,) + offset[i + 1 :]
+                self.send(src, shard, self.slots[there], self.d.peer(self.order[i], v))
+        self.send(src, shard, 16 + self.slots[offset], self.d.sibling)
+
+    def begin(self):
+        self.spread(self.own, (0,) * len(self.order), 0)
+
+    def wait(self, shard, slot):
+        ref = self.full_at(shard)
+        remote(
+            ref, ref, self.send_sems.at[0], self.recv_sems.at[slot], self.d.sibling
+        ).wait_recv()
+
+    def pass_on(self, offset):
+        shard = self.d.shard(self.order, offset, self.d.c)
+        self.wait(shard, self.slots[offset])
+        self.spread(self.full_at(shard), offset, self.last(offset) + 1)
+
+    def arrive(self):
+        for o, slot in self.slots.items():
+            self.wait(self.d.shard(self.order, o, 1 - self.d.c), 16 + slot)
+
+    def finish(self):
+        for i in range(self.sent):
+            remote(
+                self.own, self.own, self.send_sems.at[i], self.recv_sems.at[0], self.d.sibling
+            ).wait_send()
+
+
+GATHER_SEMS = 31
+
+
+def sum_refs(target, sources, step):
+    if len(target.shape) == 3:
+        for i in range(target.shape[0]):
+            sum_refs(target.at[i], [s.at[i] for s in sources], step)
+        return
+
+    def body(i, carry):
+        span = pl.ds(pl.multiple_of(i * step, step), step)
+        total = sources[0][span, :].astype(F32)
+        for source in sources[1:]:
+            total = total + source[span, :].astype(F32)
+        target[span, :] = total.astype(target.dtype)
+        return carry
+
+    lax.fori_loop(0, target.shape[0] // step, body, 0)
+
+
+class Scatter:
+    def __init__(self, d, order, part_at, own, landed, send_sems, recv_sems, total, step):
+        self.d, self.order, self.part_at, self.own, self.landed = d, order, part_at, own, landed
+        self.send_sems, self.recv_sems, self.total, self.step = send_sems, recv_sems, total, step
+        self.slots = {o: i for i, o in enumerate(offsets(order))}
+        self.lands = {}
+        for i, axis in enumerate(order):
+            for v in peers(axis):
+                for rest in offsets(order[i + 1 :]):
+                    self.lands[(i, v, rest)] = len(self.lands)
+        self.sent = 0
+        self.todo = sorted(
+            (o for o in self.slots if any(o)),
+            key=lambda o: (self.first(o), -sum(v > 0 for v in o), o),
+        )
+        self.events = [functools.partial(self.pass_on, o) for o in self.todo]
+
+    def first(self, offset):
+        return min(i for i, v in enumerate(offset) if v)
+
+    def send(self, src, dst, slot, to):
+        sem = self.send_sems.at[self.sent]
+        self.sent += 1
+        remote(src, dst, sem, self.recv_sems.at[slot], to).start()
+
+    def begin(self):
+        for o in self.todo + [(0,) * len(self.order)]:
+            slot = self.slots[o]
+            shard = self.d.shard(self.order, o, 1 - self.d.c)
+            self.send(self.part_at(shard), self.own.at[slot], slot, self.d.sibling)
+
+    def wait(self, ref, slot):
+        remote(
+            ref, ref, self.send_sems.at[0], self.recv_sems.at[slot], self.d.sibling
+        ).wait_recv()
+
+    def gathered(self, offset, until):
+        slot = self.slots[offset]
+        self.wait(self.own.at[slot], slot)
+        found = [self.own.at[slot], self.part_at(self.d.shard(self.order, offset, self.d.c))]
+        for i in range(until):
+            for v in peers(self.order[i]):
+                land = self.lands[(i, v, offset[i + 1 :])]
+                self.wait(self.landed.at[land], 16 + land)
+                found.append(self.landed.at[land])
+        return found
+
+    def pass_on(self, offset):
+        i = self.first(offset)
+        slot = self.slots[offset]
+        sum_refs(self.own.at[slot], self.gathered(offset, i), self.step)
+        land = self.lands[(i, offset[i], offset[i + 1 :])]
+        self.send(
+            self.own.at[slot],
+            self.landed.at[land],
+            16 + land,
+            self.d.peer(self.order[i], offset[i]),
+        )
+
+    def collect(self):
+        sum_refs(self.total, self.gathered((0,) * len(self.order), len(self.order)), self.step)
+
+    def finish(self):
+        ref = self.own.at[0]
+        for i in range(self.sent):
+            remote(
+                ref, ref, self.send_sems.at[i], self.recv_sems.at[0], self.d.sibling
+            ).wait_send()
+
+
+SCATTER_SEMS = 31
+
+
+def any_spec():
+    return pl.BlockSpec(memory_space=pl.ANY)
+
+
+def vmem_spec():
+    return pl.BlockSpec(memory_space=pltpu.VMEM)
+
+
+def smem_spec():
+    return pl.BlockSpec(memory_space=pltpu.SMEM)
+
+
+def shaped(shape, dtype):
+    return jax.ShapeDtypeStruct(shape, dtype)
+
+
+def vmem(shape, dtype):
+    return pltpu.VMEM(shape, dtype)
+
+
+def dma(*shape):
+    return pltpu.SemaphoreType.DMA(shape)
+
+
+def run_at(p, chunks):
+    for i, chunk in enumerate(chunks):
+        if not chunk:
+            continue
+
+        @pl.when(p == i)
+        def _(chunk=chunk):
+            for call in chunk:
+                call()
+
+
+def shared_out(calls, count):
+    per = -(-len(calls) // count)
+    return [calls[i * per : (i + 1) * per] for i in range(count)]
+
+
+def stack_head(rows, half):
+    blank = jnp.zeros_like(rows)
+    return jnp.concatenate([rows, blank] if half == 0 else [blank, rows], axis=0)
+
+
+def key_mask(mask, length):
+    row = lax.broadcasted_iota(jnp.int32, (2 * ROWS // 8, 8, 128), 0) * 8
+    row = row + lax.broadcasted_iota(jnp.int32, (2 * ROWS // 8, 8, 128), 1)
+    mask[...] = jnp.where(row.astype(F32) < length[None], 0.0, -1e30).reshape(2 * ROWS, 128)
+
+
+def front_kernel(
+    lengths, z_head, x_in, wq, wk, wv, wo, wu, bq, bv,
+    x, marks, w4, wu_full, q, qt, k, kt, v, ot, ctx, lse,
+    own4, mark, w3, vt, mask,
+    s4, r4, su, ru, sm, rm, swap_s, swap_r, pair_s, pair_r, load,
+):
+    d = Around()
+    z, c, y = d.z, d.c, d.y
+    for i, shard in enumerate((wq, wk, wv, wo)):
+        own4[i] = shard[...]
+    mark[...] = jnp.full((8, 128), lengths[0], jnp.int32).astype(F32)
+    greet(d.all)
+    swap = remote(x_in, x, swap_s.at[0], swap_r.at[0], d.across)
+
+    @pl.when(c != y)
+    def _():
+        swap.start()
+
+    def rows24(shard):
+        return w4.at[:, pl.ds(pl.multiple_of(shard * 24, 24), 24), :]
+
+    def rows96(shard):
+        return wu_full.at[pl.ds(pl.multiple_of(shard * 96, 96), 96), :]
+
+    first = Gather(d, "zyx", own4, rows24, s4, r4)
+    small = Gather(d, "zyx", mark, lambda shard: marks.at[shard], sm, rm)
+    ups = Gather(d, "zfs", wu, rows96, su, ru)
+    me = shard_of(z, d.x, c, y)
+    keep = [
+        pltpu.make_async_copy(own4, rows24(me), load.at[0]),
+        pltpu.make_async_copy(wu, rows96(me), load.at[1]),
+    ]
+    first.begin()
+    small.begin()
+    for copy in keep:
+        copy.start()
+    marks[me] = mark[...]
+
+    @pl.when(c == y)
+    def _():
+        x[...] = x_in[...]
+
+    for one, two in zip(first.events, small.events):
+        one()
+        two()
+    ups.begin()
+    keep[0].wait()
+    first.arrive()
+    load3 = [pltpu.make_async_copy(w4.at[i], w3.at[i], load.at[2 + i]) for i in range(3)]
+    for copy in load3:
+        copy.start()
+
+    @pl.when(c != y)
+    def _():
+        swap.wait()
+
+    xv = x[...]
+
+    def share(i, buf):
+        copy = remote(buf.at[c], buf.at[c], pair_s.at[i], pair_r.at[i], d.sibling)
+        copy.start()
+        return copy
+
+    load3[1].wait()
+    keys = times_trans(xv, w3[1])
+    k[c] = keys.astype(BF16)
+    copies = [share(0, k)]
+    kt[c] = keys.T.astype(BF16)
+    copies.append(share(1, kt))
+    load3[2].wait()
+    values = times_trans(xv, w3[2]) + bv[...].reshape(1, D)
+    v[c] = values.astype(BF16)
+    copies.append(share(2, v))
+    vt[c] = values.T.astype(BF16)
+    copies.append(share(3, vt))
+    load3[0].wait()
+    query = (times_trans(xv, w3[0]) + bq[...].reshape(1, D)) * SCALE
+    q[...] = query.astype(BF16)
+    qt[...] = query.T.astype(BF16)
+    small.arrive()
+    key_mask(mask, marks[z * 4 + d.x * 2 + y])
+    for i, buf in enumerate((k, kt, v, vt)):
+        remote(
+            buf.at[1 - c], buf.at[1 - c], pair_s.at[i], pair_r.at[i], d.sibling
+        ).wait_recv()
+    chunks = shared_out(ups.events, HEADS // 2)
+
+    def pair_body(p, carry):
+        run_at(p, chunks)
+        lanes = pl.ds(pl.multiple_of(p * 128, 128), 128)
+        kp = k[:, :, lanes].reshape(2 * ROWS, 128)
+        off = jnp.concatenate([mask[...]] * 4, axis=1)
+        for half in (0, 1):
+            h = p * 2 + half
+            span = pl.ds(pl.multiple_of(h * 64, 64), 64)
+            s = times_plain(kp, stack_head(qt[span, :], half)) + off
+            top = jnp.max(s, axis=0, keepdims=True)
+            e = jnp.exp(s - top)
+            den = jnp.sum(e, axis=0, keepdims=True)
+            probs = (e * (1.0 / den)).astype(BF16)
+            ot[span, :] = times_plain(vt[0, span, :], probs[:ROWS]) + times_plain(
+                vt[1, span, :], probs[ROWS:]
+            )
+            lse[pl.ds(h, 1), :] = top + jnp.log(den)
+        return carry
+
+    lax.fori_loop(0, HEADS // 2, pair_body, 0)
+    for h in range(HEADS):
+        span = slice(h * 64, h * 64 + 64)
+        ctx[:, span] = (ot[span, :] * z_head[h]).T.astype(BF16)
+    keep[1].wait()
+    ups.arrive()
+    for copy in copies:
+        copy.wait_send()
+    for gather in (first, small, ups):
+        gather.finish()
+
+
+def front(lengths, z_head, x, wq, wk, wv, wo, wu, bq, bv):
+    return pl.pallas_call(
+        front_kernel,
+        out_shape=(
+            shaped((ROWS, D), BF16),
+            shaped((32, 8, 128), F32),
+            shaped((4, D, D), BF16),
+            shaped((FF, D), BF16),
+            shaped((ROWS, D), BF16),
+            shaped((D, ROWS), BF16),
+            shaped((2, ROWS, D), BF16),
+            shaped((2, D, ROWS), BF16),
+            shaped((2, ROWS, D), BF16),
+            shaped((D, ROWS), F32),
+            shaped((ROWS, D), BF16),
+            shaped((HEADS, ROWS), F32),
+        ),
+        in_specs=[smem_spec()] * 2 + [vmem_spec()] * 8,
+        out_specs=(vmem_spec(),) * 2 + (any_spec(),) * 2 + (vmem_spec(),) * 8,
+        scratch_shapes=[
+            vmem((4, 24, D), BF16),
+            vmem((8, 128), F32),
+            vmem((3, D, D), BF16),
+            vmem((2, D, ROWS), BF16),
+            vmem((2 * ROWS, 128), F32),
+            dma(GATHER_SEMS), dma(32), dma(GATHER_SEMS), dma(32), dma(GATHER_SEMS), dma(32),
+            dma(1), dma(1), dma(4), dma(4), dma(5),
+        ],
+        compiler_params=pltpu.CompilerParams(
+            collective_id=1, has_side_effects=True, vmem_limit_bytes=60 << 20
+        ),
+        name="front",
+    )(lengths, z_head, x, wq, wk, wv, wo, wu, bq, bv)
+
+
+def rows_loop(body, step=128):
+    def run(i, carry):
+        body(i * step, pl.ds(pl.multiple_of(i * step, step), step))
+        return carry
+
+    lax.fori_loop(0, ROWS // step, run, 0)
+
+
+def col_sum(values):
+    return jnp.sum(values, axis=0, keepdims=True)
+
+
+def row_mean(values):
+    return jnp.sum(values, axis=1, keepdims=True) * (1.0 / D)
+
+
+def mid_kernel(
+    zm, zf, z_head,
+    marks, x, t_in, ctx, ot, wo, wu, wd_own, bo, bu, bd, g1, s1, g2, s2, zh, zi,
+    out, dwu, dwo, gfirst, g, gt, vec, wd_sum,
+    t, wd, dwd, attn, fn, xh1, r1, low, up, cdf, hid, gdown, acc, own_d, land_d,
+    sd, rd, ssd, rsd, swap_s, swap_r, load,
+):
+    d = Around()
+    z, c, y = d.z, d.c, d.y
+    greet(d.all)
+    gather = Gather(d, "zfs", wd_own, lambda shard: wd.at[shard], sd, rd)
+    scatter = Scatter(
+        d, "sfz", lambda shard: dwd.at[shard], own_d, land_d, ssd, rsd, wd_sum, 48
+    )
+    gather.begin()
+    wd[shard_of(z, d.x, c, y)] = wd_own[...]
+    swap = remote(t_in, t, swap_s.at[0], swap_r.at[0], d.across)
+
+    @pl.when(c != y)
+    def _():
+        swap.start()
+
+    @pl.when(c == y)
+    def _():
+        t[...] = t_in[...]
+
+    vec[...] = jnp.zeros_like(vec)
+    lane = lax.broadcasted_iota(jnp.int32, (1, D), 1)
+    row = lambda ref: ref[...].reshape(1, -1)
+
+    def add(at, value):
+        vec[at : at + 1, :] += value
+
+    def add_scalar(at, value):
+        vec[SC : SC + 1, :] += jnp.where(lane == at, value, 0.0)
+
+    attn[...] = times_plain(ctx[...], wo[...]) + row(bo)
+    ba = zm[0] * row(zh)
+    bf = zf[0] * row(zh)
+
+    def first(at, span):
+        h = x[span, :].astype(F32) + ba * attn[span, :]
+        cen = h - row_mean(h)
+        r = lax.rsqrt(row_mean(cen * cen) + epsilon)
+        xh = cen * r
+        xh1[span, :] = xh
+        r1[span, :] = jnp.broadcast_to(r, (128, 128))
+        f = xh * row(g1) + row(s1)
+        fn[span, :] = f
+        low[span, :] = f.astype(BF16)
+
+    rows_loop(first)
+    chunks = shared_out(gather.events, FF // D)
+
+    def unit_up(j, carry):
+        run_at(j, chunks)
+        units = pl.ds(pl.multiple_of(j * D, D), D)
+        u = times_trans(low[...], wu[units, :]) + bu[pl.ds(j, 1), :]
+        up[:, units] = u
+        cd = 0.5 * (1.0 + lax.erf(u * ROOT_HALF))
+        cdf[:, units] = cd
+        hid[:, units] = (u * cd * zi[pl.ds(j, 1), :]).astype(BF16)
+        return carry
+
+    lax.fori_loop(0, FF // D, unit_up, 0)
+    gather.arrive()
+    acc[...] = jnp.zeros_like(acc)
+
+    def shards(ref, j):
+        return ref[pl.ds(pl.multiple_of(j * 8, 8), 8)].reshape(D, D)
+
+    def unit_down(j, carry):
+        units = pl.ds(pl.multiple_of(j * D, D), D)
+        acc[...] += times_plain(hid[:, units], shards(wd, j))
+        return carry
+
+    lax.fori_loop(0, FF // D, unit_down, 0)
+
+    @pl.when(c != y)
+    def _():
+        swap.wait()
+
+    total = marks[0]
+    for i in range(1, 16):
+        total = total + marks[i]
+    scale = (2.0 * 32 * ROWS) / total[0:1, 0:1]
+    length = marks[z * 4 + d.x * 2 + y][0:1, 0:1]
+
+    def second(at, span):
+        down = acc[span, :] + row(bd)
+        h = fn[span, :] + bf * down
+        cen = h - row_mean(h)
+        r = lax.rsqrt(row_mean(cen * cen) + epsilon)
+        xh = cen * r
+        o = xh * row(g2) + row(s2)
+        out[span, :] = o
+        pos = lax.broadcasted_iota(jnp.int32, (128, D), 0) + (c * ROWS + at)
+        res = jnp.where(pos.astype(F32) < length, o - t[span, :].astype(F32), 0.0)
+        add_scalar(14, jnp.sum(res * res))
+        go = res * scale
+        add(G2, col_sum(go * xh))
+        add(S2, col_sum(go))
+        e = go * row(g2)
+        gs = r * (e - row_mean(e) - xh * row_mean(e * xh))
+        acc[span, :] = gs
+        gd = (gs * bf).astype(BF16)
+        gdown[span, :] = gd
+        add(BD, col_sum(gd.astype(F32)))
+        gsd = gs * down
+        add_scalar(13, jnp.sum(gsd * row(zh)))
+        add(ZH, col_sum(gsd * zf[0]))
+
+    rows_loop(second)
+
+    def down_back(j, carry):
+        units = pl.ds(pl.multiple_of(j * D, D), D)
+        dw = trans_times(hid[:, units], gdown[...]).astype(BF16)
+        dwd[pl.ds(pl.multiple_of(j * 8, 8), 8)] = dw.reshape(8, 96, D)
+        return carry
+
+    lax.fori_loop(0, FF // D, down_back, 0)
+    scatter.begin()
+    chunks_back = shared_out(scatter.events, FF // D)
+
+    def unit_back(j, carry):
+        units = pl.ds(pl.multiple_of(j * D, D), D)
+        gh = times_trans(gdown[...], shards(wd, j))
+        u = up[:, units]
+        cd = cdf[:, units]
+        vec[pl.ds(ZI + j, 1), :] = col_sum(gh * (u * cd))
+        gu = gh * zi[pl.ds(j, 1), :] * (cd + u * (DENSITY * jnp.exp(-0.5 * u * u)))
+        gu = gu.astype(BF16)
+        vec[pl.ds(BU + j, 1), :] = col_sum(gu.astype(F32))
+        acc[...] += times_plain(gu, wu[units, :])
+        dwu[units, :] = trans_times(gu, low[...]).astype(BF16)
+        run_at(j, chunks_back)
+        return carry
+
+    lax.fori_loop(0, FF // D, unit_back, 0)
+
+    def third(at, span):
+        gf = acc[span, :]
+        xh = xh1[span, :]
+        add(G1, col_sum(gf * xh))
+        add(S1, col_sum(gf))
+        e = gf * row(g1)
+        gr = r1[span, 0:1] * (e - row_mean(e) - xh * row_mean(e * xh))
+        gfirst[span, :] = gr
+        ga = (gr * ba).astype(BF16)
+        low[span, :] = ga
+        add(BO, col_sum(ga.astype(F32)))
+        gra = gr * attn[span, :]
+        add_scalar(12, jnp.sum(gra * row(zh)))
+        add(ZH, col_sum(gra * zm[0]))
+
+    rows_loop(third)
+    dwo[...] = trans_times(ctx[...], low[...]).astype(BF16)
+    gct = times_trans(wo[...], low[...])
+    for h in range(HEADS):
+        span = slice(h * 64, h * 64 + 64)
+        block = gct[span, :]
+        add_scalar(h, jnp.sum(block * ot[span, :]))
+        gb = block * z_head[h]
+        gt[span, :] = gb.astype(BF16)
+        g[:, span] = gb.T.astype(BF16)
+    scatter.collect()
+    gather.finish()
+    scatter.finish()
+
+
+def mid(zm, zf, z_head, *arrays):
+    return pl.pallas_call(
+        mid_kernel,
+        out_shape=(
+            shaped((ROWS, D), F32),
+            shaped((FF, D), BF16),
+            shaped((D, D), BF16),
+            shaped((ROWS, D), F32),
+            shaped((ROWS, D), BF16),
+            shaped((D, ROWS), BF16),
+            shaped((24, D), F32),
+            shaped((96, D), F32),
+        ),
+        in_specs=[smem_spec()] * 3 + [vmem_spec()] * len(arrays),
+        out_specs=(vmem_spec(),) * 8,
+        scratch_shapes=[
+            vmem((ROWS, D), BF16),
+            vmem((32, 96, D), BF16),
+            vmem((32, 96, D), BF16),
+            vmem((ROWS, D), F32),
+            vmem((ROWS, D), F32),
+            vmem((ROWS, D), F32),
+            vmem((ROWS, 128), F32),
+            vmem((ROWS, D), BF16),
+            vmem((ROWS, FF), F32),
+            vmem((ROWS, FF), F32),
+            vmem((ROWS, FF), BF16),
+            vmem((ROWS, D), BF16),
+            vmem((ROWS, D), F32),
+            vmem((16, 96, D), BF16),
+            vmem((15, 96, D), BF16),
+            dma(GATHER_SEMS), dma(32), dma(SCATTER_SEMS), dma(31), dma(1), dma(1), dma(1),
+        ],
+        compiler_params=pltpu.CompilerParams(
+            collective_id=2, has_side_effects=True, vmem_limit_bytes=63 << 20
+        ),
+        name="mid",
+    )(zm, zf, z_head, *arrays)
+
+
+def back_kernel(
+    marks, x, w4, q, qt, k, kt, v, g, gt, ot, lse, gfirst, vec_in, dwu, dwo, out_in,
+    gin, sum_u, sum_o, sum_q, out_swap, gin_swap, vec,
+    dqt, dkp, dvp, mask, rk, rv, w3, dw, dwo_s, own_u, land_u, own_o, land_o, own_q, land_q, va, vb, gin_low,
+    send, recv, su, ru, so, ro, sq, rq, vec_s, vec_r, swap_s, swap_r, load,
+):
+    d = Around()
+    z, c, y = d.z, d.c, d.y
+    greet(d.all)
+    swap_o = remote(out_in, out_swap, swap_s.at[0], swap_r.at[0], d.across)
+
+    @pl.when(c != y)
+    def _():
+        swap_o.start()
+
+    load3 = [pltpu.make_async_copy(w4.at[i], w3.at[i], load.at[i]) for i in range(3)]
+    for copy in load3:
+        copy.start()
+    rows96 = lambda s: dwu.at[pl.ds(pl.multiple_of(s * 96, 96), 96), :]
+    ups = Scatter(d, "sfz", rows96, own_u, land_u, su, ru, sum_u, 48)
+    outs = Scatter(d, "sfz", lambda s: dwo_s.at[s], own_o, land_o, so, ro, sum_o, 24)
+    qkv = Scatter(d, "xyz", lambda s: dw.at[:, s], own_q, land_q, sq, rq, sum_q, 24)
+    ups.begin()
+    dwo_s[...] = dwo[...].astype(F32).reshape(32, 24, D).astype(BF16)
+    outs.begin()
+    key_mask(mask, marks[z * 4 + d.x * 2 + y])
+    lane = lax.broadcasted_iota(jnp.int32, (ROWS, 128), 1)
+    chunks = shared_out([e for pair in zip(ups.events, outs.events) for e in pair], HEADS // 2)
+
+    def pair_body(p, carry):
+        lanes = pl.ds(pl.multiple_of(p * 128, 128), 128)
+        kp = k[:, :, lanes].reshape(2 * ROWS, 128)
+        vp = v[:, :, lanes].reshape(2 * ROWS, 128)
+        qp = q[:, lanes]
+        gp = g[:, lanes]
+        off = jnp.concatenate([mask[...]] * 4, axis=1)
+        zero = jnp.zeros_like(qp)
+        dka = []
+        dva = []
+        for half in (0, 1):
+            h = p * 2 + half
+            span = pl.ds(pl.multiple_of(h * 64, 64), 64)
+            mine = (lane >= 64) if half else (lane < 64)
+            s = times_plain(kp, stack_head(qt[span, :], half)) + off
+            probs = jnp.exp(s - lse[pl.ds(h, 1), :])
+            gth = gt[span, :]
+            gp_t = times_plain(vp, stack_head(gth, half))
+            dots = col_sum(gth.astype(F32) * ot[span, :])
+            ds = (probs * (gp_t - dots)).astype(BF16)
+            dka.append(times_plain(ds, jnp.where(mine, qp, zero)))
+            dva.append(times_plain(probs.astype(BF16), jnp.where(mine, gp, zero)))
+            dq = times_plain(kt[0, span, :], ds[:ROWS]) + times_plain(kt[1, span, :], ds[ROWS:])
+            dqt[span, :] = (dq * SCALE).astype(BF16)
+        dkp[:, :, lanes] = (dka[0] + dka[1]).reshape(2, ROWS, 128)
+        dvp[:, :, lanes] = (dva[0] + dva[1]).reshape(2, ROWS, 128)
+        run_at(p, chunks)
+        return carry
+
+    lax.fori_loop(0, HEADS // 2, pair_body, 0)
+    copies = [
+        remote(dkp.at[1 - c], rk, send.at[0], recv.at[0], d.sibling),
+        remote(dvp.at[1 - c], rv, send.at[1], recv.at[1], d.sibling),
+    ]
+    for copy in copies:
+        copy.start()
+
+    def keep(i, value):
+        dw[i] = value.reshape(32, 24, D).astype(BF16)
+
+    keep(0, times_plain(dqt[...], x[...]))
+    dq = dqt[...].astype(F32).T
+    va[0] = vec_in[...]
+    va[0, BQ : BQ + 1, :] = col_sum(dq)
+    for copy in copies:
+        copy.wait()
+    dk = (dkp[c] + rk[...]).astype(BF16)
+    dv = (dvp[c] + rv[...]).astype(BF16)
+    va[0, BV : BV + 1, :] = col_sum(dv.astype(F32))
+    keep(1, trans_times(dk, x[...]))
+    keep(2, trans_times(dv, x[...]))
+    qkv.begin()
+    sums = [
+        remote(va.at[i], vb.at[i], vec_s.at[i], vec_r.at[i], to)
+        for i, to in enumerate(
+            (d.sibling, d.peer("x", 1), d.peer("y", 1), d.peer("z", 1), d.peer("z", 2))
+        )
+    ]
+    sums[0].start()
+    for event in qkv.events[:2]:
+        event()
+    for copy in load3:
+        copy.wait()
+    total = gfirst[...] + times_plain(dq.astype(BF16), w3[0])
+    total = total + times_plain(dk, w3[1]) + times_plain(dv, w3[2])
+    gin[...] = total
+    gin_low[...] = total.astype(BF16)
+    swap_g = remote(gin_low, gin_swap, swap_s.at[1], swap_r.at[1], d.across)
+
+    @pl.when(c != y)
+    def _():
+        swap_g.start()
+
+    def add_up(i):
+        sums[i].wait_recv()
+        if i == 4:
+            vec[...] = va[i] + vb[i]
+        else:
+            va[i + 1] = va[i] + vb[i]
+            sums[i + 1].start()
+
+    add_up(0)
+    for i, event in enumerate(qkv.events[2:]):
+        event()
+        if i in (4, 7, 10):
+            add_up({4: 1, 7: 2, 10: 3}[i])
+    add_up(4)
+    ups.collect()
+    outs.collect()
+    qkv.collect()
+    for copy in sums:
+        copy.wait_send()
+    for scatter in (ups, outs, qkv):
+        scatter.finish()
+
+    @pl.when(c != y)
+    def _():
+        swap_o.wait()
+        swap_g.wait()
+
+
+def back(*arrays):
+    return pl.pallas_call(
+        back_kernel,
+        out_shape=(
+            shaped((ROWS, D), F32),
+            shaped((96, D), F32),
+            shaped((24, D), F32),
+            shaped((3, 24, D), F32),
+            shaped((ROWS, D), BF16),
+            shaped((ROWS, D), BF16),
+            shaped((24, D), F32),
+        ),
+        in_specs=[vmem_spec()] * 2 + [any_spec()] + [vmem_spec()] * 13 + [any_spec()],
+        out_specs=(vmem_spec(),) * 4 + (any_spec(),) * 2 + (vmem_spec(),),
+        scratch_shapes=[
+            vmem((D, ROWS), BF16),
+            vmem((2, ROWS, D), F32),
+            vmem((2, ROWS, D), F32),
+            vmem((2 * ROWS, 128), F32),
+            vmem((ROWS, D), F32),
+            vmem((ROWS, D), F32),
+            vmem((3, D, D), BF16),
+            vmem((3, 32, 24, D), BF16),
+            vmem((32, 24, D), BF16),
+            vmem((16, 96, D), BF16), vmem((15, 96, D), BF16),
+            vmem((16, 24, D), BF16), vmem((15, 24, D), BF16),
+            vmem((16, 3, 24, D), BF16), vmem((15, 3, 24, D), BF16),
+            vmem((5, 24, D), F32), vmem((5, 24, D), F32),
+            vmem((ROWS, D), BF16),
+            dma(2), dma(2),
+            dma(SCATTER_SEMS), dma(31), dma(SCATTER_SEMS), dma(31), dma(SCATTER_SEMS), dma(31),
+            dma(5), dma(5), dma(2), dma(2), dma(3),
+        ],
+        compiler_params=pltpu.CompilerParams(
+            collective_id=3, has_side_effects=True, vmem_limit_bytes=63 << 20
+        ),
+        name="back",
+    )(*arrays)
+
+
+def by_chip(
+    inputs,
+    teacher,
+    lengths,
+    w_query,
+    w_key,
+    w_value,
+    w_out,
+    w_up,
+    w_down,
+    b_query,
+    b_value,
+    b_out,
+    b_up,
+    b_down,
+    gain_one,
+    shift_one,
+    gain_two,
+    shift_two,
+    z_head,
+    z_mha,
+    z_hidden,
+    z_int,
+    z_ffn,
+):
+    z, x, core, y = place()
+    source, marks, w4, wu, q, qt, k, kt, v, ot, ctx, lse = front(
+        lengths, z_head, inputs, w_query, w_key, w_value, w_out, w_up, b_query, b_value
+    )
+    output, dwu, dwo, gfirst, g, gt, vec, sum_d = mid(
+        z_mha, z_ffn, z_head,
+        marks, source, teacher, ctx, ot, w4[3], wu, w_down, b_out, b_up.reshape(4, D), b_down,
+        gain_one, shift_one, gain_two, shift_two, z_hidden, z_int.reshape(4, D),
+    )
+    grad_inputs, sum_u, sum_o, sum_q, out_swap, grad_swap, sums = back(
+        marks, source, w4, q, qt, k, kt, v, g, gt, ot, lse, gfirst, vec, dwu, dwo,
+        output.astype(BF16),
+    )
+    home = core == y
+    layer_out = jnp.where(home, output, out_swap.astype(F32))
+    grad_home = jnp.where(home, grad_inputs, grad_swap.astype(F32))
+    valid_count = jnp.sum(marks[:16, 0, 0]).reshape(1)
+    return (
+        layer_out,
+        sums[SC, 14:15] / (D * valid_count),
+        grad_home,
+        sum_q[0],
+        sum_q[1],
+        sum_q[2],
+        sum_o,
+        sum_u,
+        sum_d,
+        sums[BQ],
+        sums[BV],
+        sums[BO],
+        sums[BU : BU + 4].reshape(-1),
+        sums[BD],
+        sums[G1],
+        sums[S1],
+        sums[G2],
+        sums[S2],
+        sums[SC, 0:12],
+        sums[SC, 12:13],
+        sums[ZH],
+        sums[ZI : ZI + 4].reshape(-1),
+        sums[SC, 13:14],
+    )
+
+
 def solution(mesh):
+    sizes = (mesh.shape["dp"], mesh.shape["tensor"])
     return jax.shard_map(
-        on_device,
+        by_chip if sizes == (16, 2) else on_device,
         mesh=mesh,
         in_specs=(
             P(("dp", "tensor"), None),

time: 976 us -> 279 us (0.29)
  waiting for transfers between devices: 537 us -> 0 us
  Pallas kernels: 0 us -> 252 us
  blocking collectives: 169 us -> 0 us
  matrix products: 129 us -> 0 us
  local copies, waits for them, and re-layouts: 59 us -> 10.1 us
  other arithmetic: 45.3 us -> 7.26 us
  between operations: 22 us -> 5.14 us
    reduce_scatter x10 -> x0, waiting for transfers between devices: 431 us -> none  [the longest x1 79.6 us: on_device(): lax.psum_scatter(grad_w_up, 'dp', scatter_dimension=0, tiled=True)]
    pallas_call x0 -> x3, Pallas kernels: none -> 252 us  [the longest x1 90.8 us: back(): pl.pallas_call(back_kernel, out_shape=(shaped((ROWS, D), F32), shaped((96...]
    dot_general x32 -> x0, matrix products: 129 us -> none  [the longest x6 39.5 us: times_trans(): lax.dot_general(left, right, (((1,), (1,)), ((), ())), preferred_element_...]
    all_gather x6 -> x0, waiting for transfers between devices: 104 us -> none  [the longest x1 27.2 us: on_device(): down_group = lax.all_gather(grad_down, 'tensor', axis=0, tiled=True)]
    psum x2 -> x0, blocking collectives: 84.6 us -> none  [on_device(): lax.psum((jnp.sum(valid_own.astype(jnp.float32)), jnp.sum(masked * masked...]
    all_gather x4 -> x0, blocking collectives: 84 us -> none  [the longest x1 23.3 us: gather_attn(): lax.all_gather(w_key, 'dp', axis=0, tiled=True)]
    dynamic_update_slice x9 -> x0, local copies, waits for them, and re-layouts: 32.9 us -> none  [the longest x4 31.6 us: forward_seq(): return lax.map(forward_block, query_seq)]
    reduce_sum x17 -> x1, other arithmetic: 30 us -> 1.46 us  [by_chip(): valid_count = jnp.sum(marks[:16, 0, 0]).reshape(1)]
  transfers between devices with their start and end apart: 16 -> 0, of which waited for: 13 -> 0; matrix products, arithmetic and copies ran while one was open for 6% -> 0% of each run, Pallas kernels for 0% -> 0%
where the time goes in v3:
time: 279 us; the launch traced here: 275 us
  Pallas kernels  252 us (90%)
  local copies, waits for them, and re-layouts  10.1 us (4%)
  other arithmetic  7.26 us (3%)
  between operations  5.14 us (2%)
    pallas_call x1, Pallas kernels, back(): pl.pallas_call(back_kernel, out_shape=(shaped((ROWS, D), F32), shaped((96...  90.8 us
    pallas_call x1, Pallas kernels, mid(): pl.pallas_call(mid_kernel, out_shape=(shaped((ROWS, D), F32), shaped((FF,...  86.9 us
    pallas_call x1, Pallas kernels, front(): pl.pallas_call(front_kernel, out_shape=(shaped((ROWS, D), BF16), shaped((...  74.6 us

profile of v3, /device:TPU:6, one launch (start us, length us, event | category | flops | bytes accessed | tf_op | source)
XLA Modules:
  0.0 274.9 jit_solution(742369183682231208)
XLA Ops:
  1.3 0.0 copy-start.5
  1.3 0.0 copy-start.6
  1.3 74.6 %front.1 = (bf16[512,768]{1,0:T(8,128)(2,1)}, f32[32,8,128]{2,1,0:T(8,128)}, bf16[4,768,768]{2,1,0:T(8,128)(2,1)}, bf16[3072,768]{1,0:T(8,128)(2,1)}, bf16[512,7...) custom-call(s32[1]{0:T(128)S(6)} %copy.49.lengths, ...), custom_call_target="tpu_custom_call" | custom-call | tf_op jit(solution)/shard_map/front/pallas_call | solution.py:723
  76.0 2.4 slice_bitcast_fusion.wo
  78.3 0.0 copy-done.5
  78.3 0.6 reshape.61.bu
  78.9 0.0 copy-done.6
  78.9 0.6 reshape.62.zi
  80.8 86.9 %mid.1 = (f32[512,768]{1,0:T(8,128)}, bf16[3072,768]{1,0:T(8,128)(2,1)}, bf16[768,768]{1,0:T(8,128)(2,1)}, f32[512,768]{1,0:T(8,128)}, bf16[512,768]{1,0:T(8,128...) custom-call(f32[1]{0:T(128)S(6)} %copy.50.zm, f32[1]{0:T(128)S(6)} %copy.51.zf, f32[12]{0:T(128)} %z_head.3, ...), custom_call_target="tpu_custom_call" | custom-call | tf_op jit(solution)/shard_map/mid/pallas_call | solution.py:944
  167.7 2.4 convert_element_type.9.out_in
  170.1 90.8 %back.1 = (f32[512,768]{1,0:T(8,128)}, f32[96,768]{1,0:T(8,128)}, f32[24,768]{1,0:T(8,128)}, f32[3,24,768]{2,1,0:T(8,128)}, bf16[512,768]{1,0:T(8,128)(2,1)}, /*...) custom-call(f32[32,8,128]{2,1,0:T(8,128)} %get-tuple-element.50.marks, bf16[512,768]{1,0:T(8,128)(2,1)} %get-tuple-element.51.x, ...), custom_call_target="tpu_custom_call" | custom-call | tf_op jit(solution)/shard_map/back/pallas_call | solution.py:1114
  260.9 1.4 fusion
  262.3 1.5 slice_reduce_fusion
  265.1 0.0 copy-start.2
  265.1 0.0 copy-start.4
  265.1 0.0 copy-start.3
  265.1 0.0 copy-start.1
  265.1 3.4 %convert_select_fusion = (f32[512,768]{1,0:T(8,128)}, f32[512,768]{1,0:T(8,128)}) fusion(f32[512,768]{1,0:T(8,128)} %get-tuple-element.71, bf16[512,768]{1,0:T(8,128)(2,1)} %get-tuple-element.72, pred[]{:T(512)S(6)} %eq.5, f32[512,768]{1,0:T(8,128)} %get-tuple-element.56, bf16[512,768]{1,0:T(8,128)(2,1)} %get-tuple-element.69), kind=kLoop, calls=%fused_computation | loop fusion | flops 1572864 | bytes 7864321 | tf_op jit(solution)/shard_map/jit(_where)/select_n | solution.py:1193
  268.6 0.0 copy-start
  268.6 0.0 copy-done.2
  268.6 0.7 slice_bitcast_fusion.1
  269.3 0.0 copy-done.4
  269.3 0.7 slice_reduce_fusion.1
  269.9 0.6 reshape.63
  270.5 0.6 reshape.64
  271.1 0.5 slice_bitcast_fusion.4
  271.7 0.0 copy-done.3
  271.7 0.6 copy.52
  272.3 0.0 copy-done.1
  272.3 0.7 copy.53
  273.0 0.0 copy-done
  273.0 0.7 copy.54
  (1 shorter events, 0.0 us)
Async XLA Ops:
  1.3 77.0 %copy-start.5 = (f32[3072]{0:T(1024)S(1)}, f32[3072]{0:T(1024)}, u32[]{:S(2)}) copy-start(f32[3072]{0:T(1024)} %param.35) | copy-start | bytes 36868
  1.3 77.6 %copy-start.6 = (f32[3072]{0:T(1024)S(1)}, f32[3072]{0:T(1024)}, u32[]{:S(2)}) copy-start(f32[3072]{0:T(1024)} %param.44) | copy-start | bytes 36868
  265.1 3.5 %copy-start.2 = (f32[3,24,768]{2,1,0:T(8,128)S(1)}, f32[3,24,768]{2,1,0:T(8,128)}, u32[]{:S(2)}) copy-start(f32[3,24,768]{2,1,0:T(8,128)} %get-tuple-element.73) | copy-start | bytes 663556
  265.1 4.2 %copy-start.4 = (f32[24,768]{1,0:T(8,128)S(1)}, f32[24,768]{1,0:T(8,128)}, u32[]{:S(2)}) copy-start(f32[24,768]{1,0:T(8,128)} %get-tuple-element.70) | copy-start | bytes 221188
  265.1 6.6 %copy-start.3 = (f32[24,768]{1,0:T(8,128)S(1)}, f32[24,768]{1,0:T(8,128)}, u32[]{:S(2)}) copy-start(f32[24,768]{1,0:T(8,128)} %get-tuple-element.125) | copy-start | bytes 221188
  265.1 7.2 %copy-start.1 = (f32[96,768]{1,0:T(8,128)S(1)}, f32[96,768]{1,0:T(8,128)}, u32[]{:S(2)}) copy-start(f32[96,768]{1,0:T(8,128)} %get-tuple-element.126) | copy-start | bytes 884740
  268.6 4.5 %copy-start = (f32[96,768]{1,0:T(8,128)S(1)}, f32[96,768]{1,0:T(8,128)}, u32[]{:S(2)}) copy-start(f32[96,768]{1,0:T(8,128)} %get-tuple-element.127) | copy-start | bytes 884740
